TPU v7x, 512 devices: a whole 4x4x16 slice. The times are simulated.
512 devices in a mesh: tm: 16 (over z), lon: 32 (over y, x, core).
Axes of the slice: x: 4, y: 4, z: 16, core: 2. Of those that a mesh axis runs over, the one named last changes fastest.
Arguments:
- noise: bfloat16 [2, 256, 1024, 512], P(None, 'tm', 'lon'), may hold values from -6 to 6
- observed: float32 [256, 256, 1024], P('tm', 'lon'), may hold values from -6 to 6
- mask: int32 [256, 256, 1024], P('tm', 'lon'), may hold values from 0 to 1, as said below
- lat_factor: bfloat16 [256, 256], replicated, as said below
- lon_factor: bfloat16 [1024, 1024], P('lon'), as said below
- spectrum: float32 [257], replicated, may hold values from 0.1 to 4
Outputs:
- posterior: float32 [2, 256, 256, 1024], P(None, 'tm', 'lon')
- residual_next: float32 [2, 256, 256, 1024], P(None, 'tm', 'lon')
Inputs may be any that keep to these rules, and one draw needn't show every extreme that they name: `mask`: 1 where the cell is observed, 0 elsewhere. `lat_factor`: lower triangular with a positive diagonal. `lon_factor`: lower triangular with a positive diagonal.
All inputs are finite; a program needn't handle non-finite values.
Results may differ from a plain program's by a relative error of at most 0.0026.
Values may be sent and summed in bfloat16 or wider, within the bound.
A program may use at most 64 MiB of HBM per device.

v0:
```python
import jax
import jax.numpy as jnp
from jax import lax
from jax.sharding import PartitionSpec as P

PRECISE = lax.Precision.HIGHEST
NOISE_VAR = 0.25


def angle_tables(row_count, col_count, period):
    row_index = lax.broadcasted_iota(jnp.int32, (row_count, col_count), 0)
    col_index = lax.broadcasted_iota(jnp.int32, (row_count, col_count), 1)
    phase = (row_index * col_index % period).astype(jnp.float32) * (2.0 * jnp.pi / period)
    return (jnp.cos(phase), jnp.sin(phase))


def over_hours(tensor_in):
    return lax.all_to_all(tensor_in, "tm", split_axis=2, concat_axis=0, tiled=True)


def over_columns(tensor_in):
    return lax.all_to_all(tensor_in, "lon", split_axis=2, concat_axis=0, tiled=True)


def finish(hourly, lat_whole, lon_forward):
    samples, hours, lat_local, lon_local = hourly.shape
    arrived = over_hours(hourly.reshape(1, samples, hours, lat_local * lon_local))
    lat_parts = arrived.shape[0]
    hour_local = arrived.shape[2]
    arrived = arrived.reshape(lat_parts, samples, hour_local, lat_local, lon_local)
    lat_split = lat_whole.reshape(lat_whole.shape[0], lat_parts, lat_local)
    spread = jnp.einsum("acy,cstyx->satx", lat_split, arrived, precision=PRECISE)
    lat_count = spread.shape[1]
    arrived = over_columns(spread.reshape(1, samples, lat_count, hour_local * lon_local))
    lon_parts = arrived.shape[0]
    lat_rows = arrived.shape[2]
    arrived = arrived.reshape(lon_parts, samples, lat_rows, hour_local, lon_local)
    return lon_forward(arrived)


def shards(noise, observed, mask, lat_factor, lon_factor, spectrum):
    periods = noise.shape[3]
    hours = periods // 2
    powers = jnp.concatenate([spectrum, spectrum[1:-1][::-1]])
    amplitude = jnp.sqrt(powers / periods)
    cosine_tab, sine_tab = angle_tables(hours, periods, periods)
    table_cos = (cosine_tab * amplitude).astype(jnp.bfloat16)
    table_sin = (sine_tab * amplitude).astype(jnp.bfloat16)
    tables = jnp.stack([jnp.stack([table_cos, table_sin]), jnp.stack([-table_sin, table_cos])])
    hourly = jnp.einsum("cyxk,scjk->sjyx", noise, tables, preferred_element_type=jnp.float32)
    scaled = powers / periods
    hour_kernel = jnp.dot(cosine_tab * scaled, cosine_tab.T, precision=PRECISE) + jnp.dot(
        sine_tab * scaled, sine_tab.T, precision=PRECISE
    )
    lat_whole = lat_factor.astype(jnp.float32)

    def lon_forward(arrived):
        lon_parts = arrived.shape[0]
        lon_local = arrived.shape[4]
        factor_rows = lax.all_gather(lon_factor, "lon", axis=0, tiled=True)
        split_rows = factor_rows.astype(jnp.float32).reshape(
            factor_rows.shape[0], lon_parts, lon_local
        )
        return jnp.einsum("odx,dsltx->stlo", split_rows, arrived, precision=PRECISE)

    prior_draw = finish(hourly, lat_whole, lon_forward)
    observed_mask = mask.astype(jnp.float32)
    residual = observed_mask * (observed[None] - prior_draw)
    local_norm = jnp.sum(residual * residual, axis=(1, 2, 3))
    norm_sq = lax.psum(local_norm, ("tm", "lon"))
    backed = jnp.einsum(
        "ij,stli->sjtl",
        lax.all_gather(lon_factor, "lon", axis=0, tiled=True).astype(jnp.float32),
        residual,
        precision=PRECISE,
    )
    samples = backed.shape[0]
    lon_count = backed.shape[1]
    hour_local = backed.shape[2]
    lat_rows = backed.shape[3]
    arrived = over_columns(backed.reshape(1, samples, lon_count, hour_local * lat_rows))
    lat_parts = arrived.shape[0]
    lon_local = arrived.shape[2]
    arrived = arrived.reshape(lat_parts, samples, lon_local, hour_local, lat_rows)
    lat_split = lat_whole.reshape(lat_parts, lat_rows, lat_whole.shape[1])
    spread = jnp.einsum("clj,csxtl->sjxt", lat_split, arrived, precision=PRECISE)
    lat_count = spread.shape[1]
    arrived = over_hours(spread.reshape(1, samples, lat_count, lon_local * hour_local))
    hour_parts = arrived.shape[0]
    lat_local = arrived.shape[2]
    arrived = arrived.reshape(hour_parts, samples, lat_local, lon_local, hour_local)
    kernel_split = hour_kernel.reshape(hour_kernel.shape[0], hour_parts, hour_local)
    hourly_back = jnp.einsum("jdt,dsyxt->sjyx", kernel_split, arrived, precision=PRECISE)
    applied = finish(hourly_back, lat_whole, lon_forward)
    operated = observed_mask * applied + NOISE_VAR * residual
    local_bend = jnp.sum(residual * operated, axis=(1, 2, 3))
    bending = lax.psum(local_bend, ("tm", "lon"))
    step_size = (norm_sq / bending)[:, None, None, None]
    return (prior_draw + step_size * applied, residual - step_size * operated)


def solution(mesh):
    return jax.shard_map(
        shards,
        mesh=mesh,
        in_specs=(
            P(None, "tm", "lon", None),
            P("tm", "lon", None),
            P("tm", "lon", None),
            P(),
            P("lon", None),
            P(),
        ),
        out_specs=(P(None, "tm", "lon", None), P(None, "tm", "lon", None)),
        check_vma=False,
    )
```

profile of v0, /device:TPU:1, one launch (start us, length us, event | category | flops | bytes accessed | tf_op | source)
XLA Modules:
  0.0 451.5 jit_solution(2240675383686566254)
XLA Ops:
  16.6 15.7 %all-to-all-start = ((f32[1,2,256,512]{3,1,0,2:T(2,128)}), f32[1,2,256,512]{3,1,0,2:T(2,128)S(1)}, u32[]{:S(2)}, u32[]{:S(2)}) async-start(f32[1,2,256,512]{3,1,0,2:T(2,128)} %copy.71), calls=%async_computation | async-start | bytes 2097152 | tf_op jit(solution)/shard_map/all_to_all | solution.py:18
  33.2 44.0 %all-to-all-done = f32[1,2,256,512]{3,1,0,2:T(2,128)S(1)} async-done(((f32[1,2,256,512]{3,1,0,2:T(2,128)}), f32[1,2,256,512]{3,1,0,2:T(2,128)S(1)}, u32[]{:S(2)}, u32[]{:S(2)}) %all-to-all-start) | async-done | bytes 1048608 | tf_op jit(solution)/shard_map/all_to_all | solution.py:18
  78.0 2.5 reshape.226
  80.5 5.8 %fusion.51 = f32[2,16,32,256,1]{3,2,4,1,0:T(8,128)S(1)} fusion(f32[16,2,16,16,32]{4,3,0,2,1:T(8,128)} %reshape.226, bf16[256,16,16,1,1]{0,2,1,4,3:T(8,128)(2,1)S(1)} %bitcast.150), kind=kOutput, calls=%fused_computation.68 | convolution fusion | flops 805306368 | bytes 2228224 | tf_op jit(solution)/shard_map/acy,cstyx->satx/dot_general | solution.py:32
  87.6 13.8 %all-to-all-start.1 = ((f32[1,2,256,512]{3,1,0,2:T(2,128)}), f32[1,2,256,512]{3,1,0,2:T(2,128)S(1)}, u32[]{:S(2)}, u32[]{:S(2)}) async-start(f32[1,2,256,512]{3,1,0,2:T(2,128)} %copy.75), calls=%async_computation.1 | async-start | bytes 2097152 | tf_op jit(solution)/shard_map/all_to_all | solution.py:22
  102.9 4.1 copy.78
  107.1 11.4 %all-to-all-done.1 = f32[1,2,256,512]{3,1,0,2:T(2,128)S(1)} async-done(((f32[1,2,256,512]{3,1,0,2:T(2,128)}), f32[1,2,256,512]{3,1,0,2:T(2,128)S(1)}, u32[]{:S(2)}, u32[]{:S(2)}) %all-to-all-start.1) | async-done | bytes 1048608 | tf_op jit(solution)/shard_map/all_to_all | solution.py:22
  119.3 2.5 reshape.229
  121.9 7.1 %subtract_multiply_fusion = (f32[2,16,8,1024]{3,1,2,0:T(8,128)S(1)}, f32[2,16,8,1024]{3,1,2,0:T(8,128)}) fusion(f32[16,8,1024]{2,0,1:T(8,128)S(1)} %copy-done.6, f32[16,8,1024]{2,0,1:T(8,128)S(1)} %copy.79, f32[32,2,8,16,32]{4,3,0,2,1:T(8,128)} %reshape.229, bf16[1024,32,32,1,1]{0,2,1,4,3:T(8,128)(2,1)} %bitcast.148), kind=kOutput, calls=%fused_computation.25 | convolution fusion | flops 3221749760 | bytes 6291456 | tf_op jit(solution)/shard_map/odx,dsltx->stlo/dot_general | solution.py:64
  131.9 20.7 %all_to_all.90 = f32[1,2,1024,128]{3,1,0,2:T(2,128)S(1)} all-to-all(f32[1,2,1024,128]{3,1,0,2:T(2,128)S(1)} %copy.82), channel_id=1, replica_groups=mesh['tm'=16,'lon'=32] {'lon'}, dimensions={2} | all-to-all | bytes 2097152 | tf_op jit(solution)/shard_map/all_to_all | solution.py:22
  152.6 2.7 copy.84
  155.3 5.7 %fusion.6 = f32[2,256,32,16]{1,2,3,0:T(8,128)S(1)} fusion(f32[32,1,2,32,128]{3,4,2,0,1:T(8,128)} %copy.84, bf16[256,256]{1,0:T(8,128)(2,1)S(1)} %copy-done.7), kind=kOutput, calls=%fused_computation.6 | convolution fusion | flops 805306368 | bytes 2228224 | tf_op jit(solution)/shard_map/clj,csxtl->sjxt/dot_general | solution.py:86
  162.9 7.9 %all-to-all-start.3 = ((f32[1,2,256,512]{3,1,0,2:T(2,128)}), f32[1,2,256,512]{3,1,0,2:T(2,128)S(1)}, u32[]{:S(2)}, u32[]{:S(2)}) async-start(f32[1,2,256,512]{3,1,0,2:T(2,128)} %copy.87), calls=%async_computation.3 | async-start | bytes 2097152 | tf_op jit(solution)/shard_map/all_to_all | solution.py:18
  170.8 2.6 fusion.19
  173.4 2.6 convolution_add_fusion
  175.9 40.2 %all-to-all-done.3 = f32[1,2,256,512]{3,1,0,2:T(2,128)S(1)} async-done(((f32[1,2,256,512]{3,1,0,2:T(2,128)}), f32[1,2,256,512]{3,1,0,2:T(2,128)S(1)}, u32[]{:S(2)}, u32[]{:S(2)}) %all-to-all-start.3) | async-done | bytes 1048608 | tf_op jit(solution)/shard_map/all_to_all | solution.py:18
  216.4 4.9 %reshape.255 = f32[16,2,16,32,16]{4,3,2,0,1:T(8,128)} reshape(f32[16,1,2,16,512]{4,3,0,2,1:T(8,128)S(1)} %bitcast.139) | data formatting | bytes 2097152 | tf_op jit(solution)/shard_map/reshape | solution.py:91
  221.2 9.3 %fusion = f32[2,16,32,256,1]{3,2,0,1,4:T(8,128)S(1)} fusion(f32[256,16,16,1,1]{0,2,3,4,1:T(8,128)S(1)} %bitcast.153, f32[16,2,16,32,16]{4,3,2,0,1:T(8,128)} %reshape.255), kind=kOutput, calls=%fused_computation | convolution fusion | flops 805306368 | bytes 2359296 | tf_op jit(solution)/shard_map/jdt,dsyxt->sjyx/dot_general | solution.py:93
  231.2 58.0 %all_to_all.91 = f32[1,2,256,512]{3,1,0,2:T(2,128)S(1)} all-to-all(f32[1,2,256,512]{3,1,0,2:T(2,128)S(1)} %copy.91), channel_id=1, replica_groups=mesh['tm'=16,'lon'=32] {'tm'}, dimensions={2} | all-to-all | bytes 2097152 | tf_op jit(solution)/shard_map/all_to_all | solution.py:18
  290.0 2.5 reshape.238
  292.5 5.7 %fusion.52 = f32[2,16,32,256,1]{3,2,4,1,0:T(8,128)S(1)} fusion(f32[16,2,16,16,32]{4,3,0,2,1:T(8,128)} %reshape.238, bf16[256,16,16,1,1]{0,2,1,4,3:T(8,128)(2,1)S(1)} %bitcast.151), kind=kOutput, calls=%fused_computation.69 | convolution fusion | flops 805306368 | bytes 2228224 | tf_op jit(solution)/shard_map/acy,cstyx->satx/dot_general | solution.py:32
  298.8 27.9 %all_to_all.92 = f32[1,2,256,512]{3,1,0,2:T(2,128)S(1)} all-to-all(f32[1,2,256,512]{3,1,0,2:T(2,128)S(1)} %copy.94), channel_id=1, replica_groups=mesh['tm'=16,'lon'=32] {'lon'}, dimensions={2} | all-to-all | bytes 2097152 | tf_op jit(solution)/shard_map/all_to_all | solution.py:22
  330.1 7.1 %multiply_reduce_fusion = (f32[2]{0:T(128)S(1)}, f32[2]{0:T(128)S(1)}, f32[2,16,8,1024]{3,1,2,0:T(8,128)}) fusion(f32[2,16,8,1024]{3,1,2,0:T(8,128)S(1)} %get-tuple-element.22, f32[16,8,1024]{2,0,1:T(8,128)S(1)} %copy-done.2, f32[32,2,8,16,32]{4,3,0,2,1:T(8,128)} %reshape.240, bf16[1024,32,32,1,1]{0,2,1,4,3:T(8,128)(2,1)} %bitcast.149), kind=kOutput, calls=%fused_computation.22 | convolution fusion | flops 3223060480 | bytes 5767184 | tf_op jit(solution)/shard_map/odx,dsltx->stlo/dot_general | solution.py:64
  337.2 102.3 %all-reduce = (f32[2]{0:T(128)S(1)}, f32[2]{0:T(128)S(1)}) all-reduce(f32[2]{0:T(128)S(1)} %get-tuple-element.11, f32[2]{0:T(128)S(1)} %get-tuple-element.10), channel_id=1, replica_groups=mesh['tm'=16,'lon'=32] {'tm','lon'}, use_global_device_ids=true, to_apply=%region_1.2 | all-reduce | flops 4 | bytes 32 | tf_op jit(solution)/shard_map/psum | solution.py:70
  (55 shorter events, 30.1 us)
Async XLA Ops:
  13.2 19.8 %copy-start.7 = (bf16[256,256]{1,0:T(8,128)(2,1)S(1)}, bf16[256,256]{1,0:T(8,128)(2,1)}, u32[]{:S(2)}) copy-start(bf16[256,256]{1,0:T(8,128)(2,1)} %param.9) | copy-start | bytes 393220
  16.6 60.6 %all-to-all-start = ((f32[1,2,256,512]{3,1,0,2:T(2,128)}), f32[1,2,256,512]{3,1,0,2:T(2,128)S(1)}, u32[]{:S(2)}, u32[]{:S(2)}) async-start(f32[1,2,256,512]{3,1,0,2:T(2,128)} %copy.71), calls=%async_computation | async-start | bytes 2097152 | tf_op jit(solution)/shard_map/all_to_all | solution.py:18
  32.3 70.6 %all-gather.2.cloned.1.call-start = ((), (), s32[]{:S(2)}) async-start(), calls=%async_computation.6 | async-start | bytes 2162688 | tf_op jit(solution)/shard_map/all_gather | solution.py:60
  80.5 20.9 %copy-start.4 = (f32[16,8,1024]{2,1,0:T(8,128)S(1)}, f32[16,8,1024]{2,1,0:T(8,128)}, u32[]{:S(2)}) copy-start(f32[16,8,1024]{2,1,0:T(8,128)} %param.7) | copy-start | bytes 1572868
  80.5 22.0 %copy-start.5 = (s32[16,8,1024]{2,1,0:T(8,128)S(1)}, s32[16,8,1024]{2,1,0:T(8,128)}, u32[]{:S(2)}) copy-start(s32[16,8,1024]{2,1,0:T(8,128)} %param.8) | copy-start | bytes 1572868
  87.6 30.9 %all-to-all-start.1 = ((f32[1,2,256,512]{3,1,0,2:T(2,128)}), f32[1,2,256,512]{3,1,0,2:T(2,128)S(1)}, u32[]{:S(2)}, u32[]{:S(2)}) async-start(f32[1,2,256,512]{3,1,0,2:T(2,128)} %copy.75), calls=%async_computation.1 | async-start | bytes 2097152 | tf_op jit(solution)/shard_map/all_to_all | solution.py:22
  102.9 19.0 %copy-start.1 = (f32[16,8,1024]{2,0,1:T(8,128)}, f32[16,8,1024]{2,0,1:T(8,128)S(1)}, u32[]{:S(2)}) copy-start(f32[16,8,1024]{2,0,1:T(8,128)S(1)} %copy.79) | copy-start | bytes 1572868
  118.7 3.2 copy-start.6
  121.8 7.1 %copy-start = (bf16[1024,1024]{1,0:T(8,128)(2,1)S(1)}, bf16[1024,1024]{1,0:T(8,128)(2,1)}, u32[]{:S(2)}) copy-start(bf16[1024,1024]{1,0:T(8,128)(2,1)} %all-gather.2.cloned.1.call-done) | copy-start | bytes 6291460
  162.9 53.3 %all-to-all-start.3 = ((f32[1,2,256,512]{3,1,0,2:T(2,128)}), f32[1,2,256,512]{3,1,0,2:T(2,128)S(1)}, u32[]{:S(2)}, u32[]{:S(2)}) async-start(f32[1,2,256,512]{3,1,0,2:T(2,128)} %copy.87), calls=%async_computation.3 | async-start | bytes 2097152 | tf_op jit(solution)/shard_map/all_to_all | solution.py:18
  326.9 3.2 copy-start.2
  330.1 109.5 %copy-start.3 = (f32[2,16,8,1024]{3,1,2,0:T(8,128)S(1)}, f32[2,16,8,1024]{3,1,2,0:T(8,128)}, u32[]{:S(2)}) copy-start(f32[2,16,8,1024]{3,1,2,0:T(8,128)} %get-tuple-element.23) | copy-start | bytes 3145732
Sparse Core Ops, SparseCore 0:
  36.3 61.1 all-gather.1
where the time goes:
time: 458 us; the launch traced here: 451 us
  blocking collectives  209 us (46%)
  waiting for transfers between devices  96.3 us (21%)
  matrix products  50.1 us (11%)
  starting transfers between devices  37.5 us (8%)
  local copies, waits for them, and re-layouts  37.2 us (8%)
  between operations  14.5 us (3%)
  other arithmetic  6.89 us (2%)
    psum x1, blocking collectives, shards(): norm_sq = lax.psum(local_norm, ('tm', 'lon'))  102 us
    all_to_all x2, waiting for transfers between devices, over_hours(): lax.all_to_all(tensor_in, 'tm', split_axis=2, concat_axis=0, tiled=True)  84.2 us
    all_to_all x1, blocking collectives, over_hours(): lax.all_to_all(tensor_in, 'tm', split_axis=2, concat_axis=0, tiled=True)  58 us
    all_to_all x2, blocking collectives, over_columns(): lax.all_to_all(tensor_in, 'lon', split_axis=2, concat_axis=0, tiled=True)  48.6 us
    all_to_all x2, starting transfers between devices, over_hours(): lax.all_to_all(tensor_in, 'tm', split_axis=2, concat_axis=0, tiled=True)  23.6 us
    dot_general x2, matrix products, lon_forward(): return jnp.einsum('odx,dsltx->stlo', split_rows, arrived, precision=PRECISE)  14.2 us
    all_to_all x1, starting transfers between devices, over_columns(): lax.all_to_all(tensor_in, 'lon', split_axis=2, concat_axis=0, tiled=True)  13.8 us
    all_to_all x1, waiting for transfers between devices, over_columns(): lax.all_to_all(tensor_in, 'lon', split_axis=2, concat_axis=0, tiled=True)  11.4 us
  transfers between devices with their start and end apart: 4, of which 3 were waited for; matrix products, arithmetic and copies ran while one was open for 5% of the time, Pallas kernels for 0%

commit v1 on v0

v1 whole, which is shorter than its diff:
```python
import functools

import jax
import jax.numpy as jnp
import numpy as np
from jax import lax
from jax.experimental import pallas as pl
from jax.experimental.pallas import tpu as pltpu
from jax.sharding import PartitionSpec as P

F32 = jnp.float32
BF16 = jnp.bfloat16
MESH = pl.DeviceIdType.MESH
NOISE_VAR = 0.25
NT = (((1,), (1,)), ((), ()))
NN = (((1,), (0,)), ((), ()))
HOPS = 8
ZN = 16
LN = 32


def dot(left, right, dims):
    return lax.dot_general(left, right, dims, preferred_element_type=F32)


def split(value):
    high = value.astype(BF16)
    return high, (value - high.astype(F32)).astype(BF16)


def exchange(parts, strides):
    parts = list(parts)
    lane = lax.broadcasted_iota(jnp.int32, parts[0].shape, 1)
    for bit, stride in enumerate(strides):
        low_lanes = (lane & stride) == 0
        for first in range(len(parts)):
            if first & (1 << bit):
                continue
            second = first | (1 << bit)
            low, high = parts[first], parts[second]
            parts[first] = jnp.where(low_lanes, low, pltpu.roll(high, stride, 1))
            parts[second] = jnp.where(low_lanes, pltpu.roll(low, 128 - stride, 1), high)
    return parts


def body(
    noise, obs_hbm, mask_hbm, lat, lon, amp, coarse, fine,
    post, nxt,
    obs, mask, tab, waves, work, ysc, ssc, lat32, latp, latq, latqt, hour,
    lonfull, halves, xd, prior, resid,
    send0, recv0, send1, recv1, send2, recv2, send3, recv3, send4, recv4, send5, recv5,
    redsend, redz, redmid, redl,
    send_sem, recv_sem, local_sem,
):
    mz = lax.axis_index("tm")
    ml = lax.axis_index("lon")

    def z_peer(step):
        away = (step // 2 + 1) * (1 - 2 * (step % 2))
        return lax.rem(mz + away + ZN, ZN)

    def l_peer(step):
        return lax.rem(ml + step + 1, LN)

    barrier = pltpu.get_barrier_semaphore()

    def greet_z(step, carry):
        pl.semaphore_signal(barrier, inc=1, device_id={"tm": z_peer(step)}, device_id_type=MESH)
        return carry

    def greet_l(step, carry):
        pl.semaphore_signal(barrier, inc=1, device_id={"lon": l_peer(step)}, device_id_type=MESH)
        return carry

    lax.fori_loop(0, ZN - 1, greet_z, 0)
    lax.fori_loop(0, LN - 1, greet_l, 0)
    obs_copy = pltpu.make_async_copy(obs_hbm, obs, local_sem.at[0])
    mask_copy = pltpu.make_async_copy(mask_hbm, mask, local_sem.at[1])
    obs_copy.start()
    mask_copy.start()

    def start_z(hop, s, src, dst):
        def one(step, carry):
            peer = z_peer(step)
            pltpu.make_async_remote_copy(
                src_ref=src.at[s, peer], dst_ref=dst.at[s, mz],
                send_sem=send_sem.at[hop, s], recv_sem=recv_sem.at[hop, s],
                device_id={"tm": peer}, device_id_type=MESH,
            ).start()
            return carry

        lax.fori_loop(0, ZN - 1, one, 0)
        dst[s, mz] = src[s, mz]

    def whole_z(hop, s, src, dst):
        return pltpu.make_async_remote_copy(
            src_ref=src.at[s, pl.ds(0, ZN - 1)], dst_ref=dst.at[s, pl.ds(0, ZN - 1)],
            send_sem=send_sem.at[hop, s], recv_sem=recv_sem.at[hop, s],
            device_id={"tm": z_peer(0)}, device_id_type=MESH,
        )

    def start_l(hop, s, src, dst):
        def one(step, carry):
            peer = l_peer(step)
            pltpu.make_async_remote_copy(
                src_ref=src.at[s, pl.ds(pl.multiple_of(peer * 32, 32), 32)],
                dst_ref=dst.at[s, pl.ds(pl.multiple_of(ml * 32, 32), 32)],
                send_sem=send_sem.at[hop, s], recv_sem=recv_sem.at[hop, s],
                device_id={"lon": peer}, device_id_type=MESH,
            ).start()
            return carry

        lax.fori_loop(0, LN - 1, one, 0)
        own = pl.ds(pl.multiple_of(ml * 32, 32), 32)
        dst[s, own] = src[s, own]

    def whole_l(hop, s, src, dst):
        rows = pl.ds(0, (LN - 1) * 32)
        return pltpu.make_async_remote_copy(
            src_ref=src.at[s, rows], dst_ref=dst.at[s, rows],
            send_sem=send_sem.at[hop, s], recv_sem=recv_sem.at[hop, s],
            device_id={"lon": l_peer(0)}, device_id_type=MESH,
        )

    amp_row = amp[...]

    def tables(group):
        base = pl.multiple_of(group * 8, 8)
        c1 = coarse[pl.ds(base, 8), :]
        s1 = coarse[pl.ds(16 + base, 8), :]
        for pair in range(8):
            cos_rows, sin_rows = [], []
            for hh in (2 * pair, 2 * pair + 1):
                c2, s2 = fine[hh : hh + 1, :], fine[16 + hh : 17 + hh, :]
                cos_rows.append((c1 * c2 - s1 * s2) * amp_row)
                sin_rows.append((s1 * c2 + c1 * s2) * amp_row)
            cw = jnp.concatenate(cos_rows, axis=0).astype(BF16)
            sw = jnp.concatenate(sin_rows, axis=0).astype(BF16)
            rows = pl.ds(pair * 16, 16)
            tab[0, group, rows, 0:512] = cw
            tab[0, group, rows, 512:1024] = sw
            tab[1, group, rows, 0:512] = -sw
            tab[1, group, rows, 512:1024] = cw

    def tables_loop(group, carry):
        tables(group)
        return carry

    lax.fori_loop(0, 2, tables_loop, 0)

    def transform(s):
        def one(group, carry):
            for part in range(2):
                rows = noise[part].reshape(512, 512)
                term = dot(rows, tab[s, group, :, part * 512 : (part + 1) * 512], NT)
                if part == 0:
                    work[0:512, :] = term
                else:
                    work[0:512, :] += term

            def swap(u, inner):
                parts = [work[pl.ds(u * 8 + og, 16, stride=32), :] for og in range(8)]
                parts = exchange(parts, (1, 2, 4))
                for jl in range(8):
                    send0[s, group * 8 + jl, u] = parts[jl].astype(BF16)
                return inner

            lax.fori_loop(0, 4, swap, 0)
            return carry

        lax.fori_loop(0, 2, one, 0)

    transform(0)
    pl.semaphore_wait(barrier, ZN + LN - 2)
    start_z(0, 0, send0, recv0)

    own_rows = pl.ds(pl.multiple_of(ml * 32, 32), 32)

    def gather(step, carry):
        pltpu.make_async_remote_copy(
            src_ref=lon, dst_ref=lonfull.at[own_rows],
            send_sem=local_sem.at[2], recv_sem=local_sem.at[3],
            device_id={"lon": l_peer(step)}, device_id_type=MESH,
        ).start()
        return carry

    lax.fori_loop(0, LN - 1, gather, 0)
    lonfull[own_rows, :] = lon[...]
    gathered = pltpu.make_async_remote_copy(
        src_ref=lonfull.at[pl.ds(0, 31 * 32)], dst_ref=lonfull.at[pl.ds(0, 31 * 32)],
        send_sem=local_sem.at[2], recv_sem=local_sem.at[3],
        device_id={"lon": l_peer(0)}, device_id_type=MESH,
    )
    transform(1)
    start_z(0, 1, send0, recv0)

    def spread(value):
        lat32[0:256, :] = value[:, 0:128]
        lat32[256:512, :] = value[:, 128:256]

    spread(lat[...].astype(F32))
    for k in range(8):
        latp[k * 32 : (k + 1) * 32, :] = jnp.concatenate(
            [lat32[pl.ds(c * 256 + k, 32, stride=8), :] for c in range(2)], axis=1
        ).astype(BF16)
    spread(latp[...].astype(F32).T)
    for bb in range(16):
        latqt[bb * 16 : (bb + 1) * 16, :] = jnp.concatenate(
            [lat32[pl.ds(c * 256 + bb, 16, stride=16), :] for c in range(2)], axis=1
        ).astype(BF16)
    latq[...] = latqt[...].astype(F32).T.astype(BF16)

    def wave(j, carry):
        c1 = coarse[pl.ds(j, 1), :] * amp_row
        s1 = coarse[pl.ds(16 + j, 1), :] * amp_row
        c2, s2 = fine[0:16, :], fine[16:32, :]
        rows = pl.ds(pl.multiple_of(j * 16, 16), 16)
        for part, value in enumerate((c1 * c2 - s1 * s2, s1 * c2 + c1 * s2)):
            high, low = split(value)
            waves[0, rows, part * 512 : (part + 1) * 512] = high
            waves[1, rows, part * 512 : (part + 1) * 512] = low
        return carry

    lax.fori_loop(0, ZN, wave, 0)
    cross = dot(waves[0], waves[1], NT)
    kernel = dot(waves[0], waves[0], NT) + (cross + cross.T)
    high, low = split(kernel)
    hour[0:256, :] = high
    hour[256:512, :] = low
    redsend[...] = jnp.zeros_like(redsend)
    obs_copy.wait()
    mask_copy.wait()

    def columns(index, width):
        return pl.ds(pl.multiple_of(index * width, width), width)

    def to_lon(s, dst):
        def swap(step, carry):
            u, lb = step // 2, step % 2
            parts = [
                ysc[pl.ds(pl.multiple_of(k * 32 + lb * 16, 16), 16), columns(u, 128)] for k in range(8)
            ]
            parts = exchange(parts, (1, 2, 4))
            for og in range(8):
                ssc[pl.ds(pl.multiple_of((u * 8 + og) * 32 + lb * 16, 16), 16), :] = parts[og]
            return carry

        lax.fori_loop(0, 8, swap, 0)

        def pick(peer, carry):
            dst[s, pl.ds(pl.multiple_of(peer * 32, 32), 32), :] = ssc[pl.ds(peer, 32, stride=32), :]
            return carry

        lax.fori_loop(0, LN, pick, 0)

    def lat_first(s):
        whole_z(0, s, send0, recv0).wait_recv()
        for u in range(4):
            ysc[:, u * 128 : (u + 1) * 128] = dot(latp[...], recv0[s, :, u].reshape(256, 128), NN)
        to_lon(s, send1)
        start_l(1, s, send1, recv1)

    def lon_columns(s, src):
        def turn(c, carry):
            block = src[s, columns(c, 128), :].T
            high, low = split(block)
            halves[0:128, columns(c, 128)] = high
            halves[128:256, columns(c, 128)] = low
            return carry

        lax.fori_loop(0, 8, turn, 0)

    def lon_first(s):
        whole_l(1, s, send1, recv1).wait_recv()
        lon_columns(s, recv1)

        def prior_block(n, total):
            both = dot(halves[...], lonfull[columns(n, 256), :], NT)
            drawn = both[0:128] + both[128:256]
            left = mask[:, columns(n, 256)].astype(F32) * (obs[:, columns(n, 256)] - drawn)
            prior[s, :, columns(n, 256)] = drawn
            resid[s, :, columns(n, 256)] = left
            squares = jnp.sum(left * left, axis=0, keepdims=True)
            return total + squares[:, 0:128] + squares[:, 128:256]

        redsend[s, 0:1, :] = lax.fori_loop(0, 4, prior_block, jnp.zeros((1, 128), F32))

        def halve(n, carry):
            high, low = split(resid[s, :, columns(n, 256)])
            halves[0:128, columns(n, 256)] = high
            halves[128:256, columns(n, 256)] = low
            return carry

        lax.fori_loop(0, 4, halve, 0)

        def back_block(n, carry):
            both = dot(halves[...], lonfull[:, columns(n, 256)], NN)
            summed = both[0:128] + both[128:256]
            for part in range(2):
                rows = pl.ds(pl.multiple_of(n * 256 + part * 128, 128), 128)
                send2[s, rows, :] = summed[:, part * 128 : (part + 1) * 128].T
            return carry

        lax.fori_loop(0, 4, back_block, 0)
        start_l(2, s, send2, recv2)

    def lat_back(s):
        whole_l(2, s, send2, recv2).wait_recv()

        def swap(step, carry):
            u, lb = step // 2, step % 2
            parts = [recv2[s, pl.ds(lb * 512 + u * 8 + pg, 16, stride=32), :] for pg in range(8)]
            parts = exchange(parts, (1, 2, 4))
            for k in range(8):
                high, low = split(parts[k])
                rows = pl.ds(pl.multiple_of(k * 32 + lb * 16, 16), 16)
                xd[0, rows, columns(u, 128)] = high
                xd[1, rows, columns(u, 128)] = low
            return carry

        lax.fori_loop(0, 8, swap, 0)
        for n in range(2):
            cols = slice(n * 256, (n + 1) * 256)
            ysc[:, cols] = dot(latqt[...], xd[0, :, cols], NN) + dot(latqt[...], xd[1, :, cols], NN)

        def turn(step, carry):
            u, ib = step // 2, step % 2
            parts = [ysc[pl.ds(pl.multiple_of(bb * 16 + ib * 8, 8), 8), columns(u, 128)] for bb in range(16)]
            parts = exchange(parts, (8, 16, 32, 64))
            for h in range(16):
                ssc[pl.ds(pl.multiple_of((u * 16 + h) * 16 + ib * 8, 8), 8), :] = parts[h]
            return carry

        lax.fori_loop(0, 8, turn, 0)

        def pick(peer, carry):
            for u in range(4):
                send3[s, peer, u] = ssc[pl.ds(u * 256 + peer, 16, stride=16), :].astype(BF16)
            return carry

        lax.fori_loop(0, ZN, pick, 0)
        start_z(3, s, send3, recv3)

    def hours_mix(s):
        whole_z(3, s, send3, recv3).wait_recv()
        total = jnp.zeros((1, 128), F32)
        for u in range(4):
            cells = recv3[s, :, u].reshape(256, 128)
            both = dot(hour[...], cells, NN)
            mixed = both[0:256] + both[256:512]
            total = total + jnp.sum(mixed * cells.astype(F32), axis=0, keepdims=True)
            send4[s, :, u] = mixed.astype(BF16).reshape(16, 16, 128)
        redsend[s, 1:2, :] = total

        def one(step, carry):
            peer = z_peer(step)
            pltpu.make_async_remote_copy(
                src_ref=redsend.at[s], dst_ref=redz.at[s, mz],
                send_sem=send_sem.at[6, s], recv_sem=recv_sem.at[6, s],
                device_id={"tm": peer}, device_id_type=MESH,
            ).start()
            return carry

        lax.fori_loop(0, ZN - 1, one, 0)
        redz[s, mz] = redsend[s]
        start_z(4, s, send4, recv4)

    def sums_lon(s):
        whole_z(6, s, redz, redz).wait_recv()
        redmid[s] = jnp.sum(redz[s], axis=0)

        def one(step, carry):
            pltpu.make_async_remote_copy(
                src_ref=redmid.at[s], dst_ref=redl.at[s, ml],
                send_sem=send_sem.at[7, s], recv_sem=recv_sem.at[7, s],
                device_id={"lon": l_peer(step)}, device_id_type=MESH,
            ).start()
            return carry

        lax.fori_loop(0, LN - 1, one, 0)
        redl[s, ml] = redmid[s]

    def sums_whole(s):
        part = redl.at[s, pl.ds(0, LN - 1)]
        return pltpu.make_async_remote_copy(
            src_ref=part, dst_ref=part, send_sem=send_sem.at[7, s], recv_sem=recv_sem.at[7, s],
            device_id={"lon": l_peer(0)}, device_id_type=MESH,
        )

    def lat_last(s):
        whole_z(4, s, send4, recv4).wait_recv()

        def widen(i, carry):
            ssc[pl.ds(pl.multiple_of(i * 64, 64), 64), :] = recv4[s, i].reshape(64, 128).astype(F32)
            return carry

        lax.fori_loop(0, ZN, widen, 0)

        def turn(u, carry):
            parts = [ssc[pl.ds(u * 16 + h, 16, stride=64), :] for h in range(16)]
            parts = exchange(parts, (8, 16, 32, 64))
            for bb in range(16):
                xd[0, pl.ds(bb * 16, 16), columns(u, 128)] = parts[bb].astype(BF16)
            return carry

        lax.fori_loop(0, 4, turn, 0)
        for n in range(2):
            cols = slice(n * 256, (n + 1) * 256)
            ysc[:, cols] = dot(latq[...], xd[0, :, cols], NN)
        to_lon(s, send5)
        start_l(5, s, send5, recv5)

    def lon_last(s):
        sums_whole(s).wait_recv()
        total = jnp.sum(redl[s], axis=0)
        norm_sq = jnp.sum(total[0:1], axis=1, keepdims=True)
        quad = jnp.sum(total[1:2], axis=1, keepdims=True)
        step_size = norm_sq / (quad + NOISE_VAR * norm_sq)
        whole_l(5, s, send5, recv5).wait_recv()
        lon_columns(s, recv5)

        def block(n, carry):
            both = dot(halves[...], lonfull[columns(n, 256), :], NT)
            applied = both[0:128] + both[128:256]
            left = resid[s, :, columns(n, 256)]
            operated = mask[:, columns(n, 256)].astype(F32) * applied + NOISE_VAR * left
            post[s, :, columns(n, 256)] = prior[s, :, columns(n, 256)] + step_size * applied
            nxt[s, :, columns(n, 256)] = left - step_size * operated
            return carry

        lax.fori_loop(0, 4, block, 0)

    lat_first(0)
    gathered.wait_recv()
    lon_first(0)
    lat_first(1)
    lat_back(0)
    lon_first(1)
    lat_back(1)
    hours_mix(0)
    hours_mix(1)
    sums_lon(0)
    sums_lon(1)
    lat_last(0)
    lon_last(0)
    lat_last(1)
    lon_last(1)

    gathered.wait_send()
    for s in range(2):
        whole_z(0, s, send0, recv0).wait_send()
        whole_l(1, s, send1, recv1).wait_send()
        whole_l(2, s, send2, recv2).wait_send()
        whole_z(3, s, send3, recv3).wait_send()
        whole_z(4, s, send4, recv4).wait_send()
        whole_l(5, s, send5, recv5).wait_send()
        whole_z(6, s, redz, redz).wait_send()
        sums_whole(s).wait_send()


def trig(step, period, count, columns):
    angle = 2.0 * np.pi * ((step * np.arange(count)[:, None] * np.arange(columns)[None]) % period) / period
    return np.concatenate([np.cos(angle), np.sin(angle)]).astype(np.float32)


def shards(noise, observed, mask, lat_factor, lon_factor, spectrum):
    periods = noise.shape[3]
    powers = jnp.concatenate([spectrum, spectrum[1:-1][::-1]])
    amplitude = jnp.sqrt(powers / periods)[None]
    coarse = jnp.asarray(trig(16, 512, 16, 512))
    fine = jnp.asarray(trig(1, 512, 16, 512))
    vmem = pl.BlockSpec(memory_space=pltpu.VMEM)
    anywhere = pl.BlockSpec(memory_space=pl.ANY)
    zbuf = pltpu.VMEM((2, 16, 4, 16, 128), BF16)
    lbuf = pltpu.VMEM((2, 1024, 128), F32)
    scratch = [
        pltpu.VMEM((128, 1024), F32),
        pltpu.VMEM((128, 1024), jnp.int32),
        pltpu.VMEM((2, 2, 128, 1024), BF16),
        pltpu.VMEM((2, 256, 1024), BF16),
        pltpu.VMEM((512, 128), F32),
        pltpu.VMEM((256, 512), F32),
        pltpu.VMEM((1024, 128), F32),
        pltpu.VMEM((512, 128), F32),
        pltpu.VMEM((256, 256), BF16),
        pltpu.VMEM((256, 256), BF16),
        pltpu.VMEM((256, 256), BF16),
        pltpu.VMEM((512, 256), BF16),
        pltpu.VMEM((1024, 1024), BF16),
        pltpu.VMEM((256, 1024), BF16),
        pltpu.VMEM((2, 256, 512), BF16),
        pltpu.VMEM((2, 128, 1024), F32),
        pltpu.VMEM((2, 128, 1024), F32),
        zbuf, zbuf, lbuf, lbuf, lbuf, lbuf, zbuf, zbuf, zbuf, zbuf, lbuf, lbuf,
        pltpu.VMEM((2, 8, 128), F32),
        pltpu.VMEM((2, 16, 8, 128), F32),
        pltpu.VMEM((2, 8, 128), F32),
        pltpu.VMEM((2, 32, 8, 128), F32),
        pltpu.SemaphoreType.DMA((HOPS, 2)),
        pltpu.SemaphoreType.DMA((HOPS, 2)),
        pltpu.SemaphoreType.DMA((4,)),
    ]
    out = jax.ShapeDtypeStruct((2, 128, 1024), F32)
    post, nxt = pl.pallas_call(
        body,
        out_shape=(out, out),
        in_specs=[vmem, anywhere, anywhere, vmem, vmem, vmem, vmem, vmem],
        out_specs=(vmem, vmem),
        scratch_shapes=scratch,
        compiler_params=pltpu.CompilerParams(
            collective_id=0, has_side_effects=True, vmem_limit_bytes=50 << 20
        ),
        name="posterior",
    )(
        noise, observed.reshape(128, 1024), mask.reshape(128, 1024), lat_factor, lon_factor, amplitude, coarse, fine
    )
    return post.reshape(2, 16, 8, 1024), nxt.reshape(2, 16, 8, 1024)


def solution(mesh):
    return jax.shard_map(
        shards,
        mesh=mesh,
        in_specs=(
            P(None, "tm", "lon", None),
            P("tm", "lon", None),
            P("tm", "lon", None),
            P(),
            P("lon", None),
            P(),
        ),
        out_specs=(P(None, "tm", "lon", None), P(None, "tm", "lon", None)),
        check_vma=False,
    )
```

time: 458 us -> 166 us (0.36); the launches traced: 451 us -> 166 us
  blocking collectives: 209 us -> 0 us
  Pallas kernels: 0 us -> 157 us
  waiting for transfers between devices: 96.3 us -> 0 us
  matrix products: 50.1 us -> 0 us
  starting transfers between devices: 37.5 us -> 0 us
  local copies, waits for them, and re-layouts: 37.2 us -> 8.37 us
  between operations: 14.5 us -> 0.66 us
  other arithmetic: 6.89 us -> 0.08 us
    pallas_call x0 -> x1, Pallas kernels: none -> 157 us  [shards(): pl.pallas_call(body, out_shape=(out, out), in_specs=[vmem, anywhere, anyw...]
    all_to_all x3 -> x0, blocking collectives: 107 us -> none  [the longest x1 58 us: over_hours(): lax.all_to_all(tensor_in, 'tm', split_axis=2, concat_axis=0, tiled=True)]
    psum x1 -> x0, blocking collectives: 102 us -> none  [shards(): norm_sq = lax.psum(local_norm, ('tm', 'lon'))]
    all_to_all x3 -> x0, waiting for transfers between devices: 95.6 us -> none  [the longest x2 84.2 us: over_hours(): lax.all_to_all(tensor_in, 'tm', split_axis=2, concat_axis=0, tiled=True)]
    dot_general x10 -> x0, matrix products: 50.1 us -> none  [the longest x2 14.2 us: lon_forward(): return jnp.einsum('odx,dsltx->stlo', split_rows, arrived, precision=PRECISE)]
    all_to_all x3 -> x0, starting transfers between devices: 37.4 us -> none  [the longest x2 23.6 us: over_hours(): lax.all_to_all(tensor_in, 'tm', split_axis=2, concat_axis=0, tiled=True)]
    reshape x11 -> x0, local copies, waits for them, and re-layouts: 20.6 us -> none  [the longest x2 5.05 us: finish(): arrived.reshape(lat_parts, samples, hour_local, lat_local, lon_local)]
    all_to_all x11 -> x0, local copies, waits for them, and re-layouts: 6.19 us -> none  [the longest x6 4.36 us: over_columns(): lax.all_to_all(tensor_in, 'lon', split_axis=2, concat_axis=0, tiled=True)]
  transfers between devices with their start and end apart: 4 -> 0, of which waited for: 3 -> 0; matrix products, arithmetic and copies ran while one was open for 5% -> 0% of each run, Pallas kernels for 0% -> 0%
where the time goes in v1:
time: 166 us
  Pallas kernels  157 us (95%)
  local copies, waits for them, and re-layouts  8.37 us (5%)
    pallas_call x1, Pallas kernels, shards(): pl.pallas_call(body, out_shape=(out, out), in_specs=[vmem, anywhere, anyw...  157 us
    unnamed x18, local copies, waits for them, and re-layouts  8.29 us

profile of v1, /device:TPU:1, one launch (start us, length us, event | category | flops | bytes accessed | tf_op | source)
XLA Modules:
  0.0 165.8 jit_solution(10231403794117411978)
XLA Ops:
  0.6 0.0 copy-start.6
  0.6 0.7 copy-done.6
  1.3 0.1 slice.3
  1.4 0.1 reverse
  1.5 0.1 slice.4
  1.6 0.1 fusion.amp
  1.6 0.0 copy-start
  1.6 1.0 copy-done
  2.7 0.0 copy-start.1
  2.7 1.0 copy-done.1
  3.7 0.0 copy-start.2
  3.7 0.9 copy-done.2
  4.6 0.0 copy-start.3
  4.6 0.8 copy-done.3
  5.5 0.0 copy-start.4
  5.5 0.8 copy-done.4
  6.3 0.0 copy-start.5
  6.3 0.8 copy-done.5
  7.2 156.7 %posterior.1 = (f32[2,128,1024]{2,1,0:T(8,128)S(1)}, f32[2,128,1024]{2,1,0:T(8,128)S(1)}) custom-call(bf16[2,16,32,512]{3,2,1,0:T(8,128)(2,1)} %noise.1, f32[128,1024]{1,0:T(8,128)S(1)} %bitcast.8, s32[128,1024]{1,0:T(8,128)S(1)} %bitcast.9, bf16[256,256]{1,0:T(8,128)(2,1)S(1)} %copy-done.2, bf16[32,1024]{1,0:T(8,128)(2,1)S(1)} %copy-done.3, ...), custom_call_target="tpu_custom_call" | custom-call | tf_op jit(solution)/shard_map/posterior/pallas_call | solution.py:504
  163.8 1.0 copy.12
  164.8 1.0 copy.13
  (1 shorter events, 0.0 us)
Async XLA Ops:
  0.6 0.7 copy-start.6
  1.6 1.0 copy-start
  2.7 1.0 copy-start.1
  3.7 0.9 copy-start.2
  4.6 0.8 copy-start.3
  5.5 0.8 copy-start.4
  6.3 0.8 copy-start.5

commit v2 on v1

--- a/solution.py
+++ b/solution.py
@@ -17,6 +17,10 @@
 HOPS = 8
 ZN = 16
 LN = 32
+
+
+def repeat(count, step):
+    lax.fori_loop(0, count, step, 0, unroll=min(count, 8))
 
 
 def dot(left, right, dims):
@@ -44,9 +48,9 @@
 
 
 def body(
-    noise, obs_hbm, mask_hbm, lat, lon, amp, coarse, fine,
+    noise_hbm, obs_hbm, mask_hbm, lat_hbm, lon_hbm, amp, coarse_hbm, fine_hbm,
     post, nxt,
-    obs, mask, tab, waves, work, ysc, ssc, lat32, latp, latq, latqt, hour,
+    noise, lat, lon, coarse, fine, obs, mask, tab, waves, work, ysc, ssc, lat32, latp, latq, latqt, hour,
     lonfull, halves, xd, prior, resid,
     send0, recv0, send1, recv1, send2, recv2, send3, recv3, send4, recv4, send5, recv5,
     redsend, redz, redmid, redl,
@@ -62,6 +66,15 @@
     def l_peer(step):
         return lax.rem(ml + step + 1, LN)
 
+    fetches = [
+        pltpu.make_async_copy(src, dst, local_sem.at[index])
+        for index, (src, dst) in enumerate(
+            [(coarse_hbm, coarse), (fine_hbm, fine), (noise_hbm, noise), (lat_hbm, lat), (lon_hbm, lon),
+             (obs_hbm, obs), (mask_hbm, mask)]
+        )
+    ]
+    for fetch in fetches:
+        fetch.start()
     barrier = pltpu.get_barrier_semaphore()
 
     def greet_z(step, carry):
@@ -74,10 +87,6 @@
 
     lax.fori_loop(0, ZN - 1, greet_z, 0)
     lax.fori_loop(0, LN - 1, greet_l, 0)
-    obs_copy = pltpu.make_async_copy(obs_hbm, obs, local_sem.at[0])
-    mask_copy = pltpu.make_async_copy(mask_hbm, mask, local_sem.at[1])
-    obs_copy.start()
-    mask_copy.start()
 
     def start_z(hop, s, src, dst):
         def one(step, carry):
@@ -122,6 +131,8 @@
             device_id={"lon": l_peer(0)}, device_id_type=MESH,
         )
 
+    for fetch in fetches[:5]:
+        fetch.wait()
     amp_row = amp[...]
 
     def tables(group):
@@ -165,34 +176,13 @@
                     send0[s, group * 8 + jl, u] = parts[jl].astype(BF16)
                 return inner
 
-            lax.fori_loop(0, 4, swap, 0)
+            repeat(4, swap)
             return carry
 
         lax.fori_loop(0, 2, one, 0)
 
     transform(0)
-    pl.semaphore_wait(barrier, ZN + LN - 2)
-    start_z(0, 0, send0, recv0)
-
-    own_rows = pl.ds(pl.multiple_of(ml * 32, 32), 32)
-
-    def gather(step, carry):
-        pltpu.make_async_remote_copy(
-            src_ref=lon, dst_ref=lonfull.at[own_rows],
-            send_sem=local_sem.at[2], recv_sem=local_sem.at[3],
-            device_id={"lon": l_peer(step)}, device_id_type=MESH,
-        ).start()
-        return carry
-
-    lax.fori_loop(0, LN - 1, gather, 0)
-    lonfull[own_rows, :] = lon[...]
-    gathered = pltpu.make_async_remote_copy(
-        src_ref=lonfull.at[pl.ds(0, 31 * 32)], dst_ref=lonfull.at[pl.ds(0, 31 * 32)],
-        send_sem=local_sem.at[2], recv_sem=local_sem.at[3],
-        device_id={"lon": l_peer(0)}, device_id_type=MESH,
-    )
     transform(1)
-    start_z(0, 1, send0, recv0)
 
     def spread(value):
         lat32[0:256, :] = value[:, 0:128]
@@ -228,9 +218,29 @@
     hour[0:256, :] = high
     hour[256:512, :] = low
     redsend[...] = jnp.zeros_like(redsend)
-    obs_copy.wait()
-    mask_copy.wait()
-
+    fetches[5].wait()
+    fetches[6].wait()
+
+    pl.semaphore_wait(barrier, ZN + LN - 2)
+    start_z(0, 0, send0, recv0)
+
+    own_rows = pl.ds(pl.multiple_of(ml * 32, 32), 32)
+
+    def gather(step, carry):
+        pltpu.make_async_remote_copy(
+            src_ref=lon, dst_ref=lonfull.at[own_rows],
+            send_sem=local_sem.at[7], recv_sem=local_sem.at[8],
+            device_id={"lon": l_peer(step)}, device_id_type=MESH,
+        ).start()
+        return carry
+
+    lax.fori_loop(0, LN - 1, gather, 0)
+    lonfull[own_rows, :] = lon[...]
+    gathered = pltpu.make_async_remote_copy(
+        src_ref=lonfull.at[pl.ds(0, 31 * 32)], dst_ref=lonfull.at[pl.ds(0, 31 * 32)],
+        send_sem=local_sem.at[7], recv_sem=local_sem.at[8],
+        device_id={"lon": l_peer(0)}, device_id_type=MESH,
+    )
     def columns(index, width):
         return pl.ds(pl.multiple_of(index * width, width), width)
 
@@ -245,16 +255,18 @@
                 ssc[pl.ds(pl.multiple_of((u * 8 + og) * 32 + lb * 16, 16), 16), :] = parts[og]
             return carry
 
-        lax.fori_loop(0, 8, swap, 0)
+        repeat(8, swap)
 
         def pick(peer, carry):
             dst[s, pl.ds(pl.multiple_of(peer * 32, 32), 32), :] = ssc[pl.ds(peer, 32, stride=32), :]
             return carry
 
-        lax.fori_loop(0, LN, pick, 0)
+        repeat(LN, pick)
 
     def lat_first(s):
         whole_z(0, s, send0, recv0).wait_recv()
+        if s == 0:
+            start_z(0, 1, send0, recv0)
         for u in range(4):
             ysc[:, u * 128 : (u + 1) * 128] = dot(latp[...], recv0[s, :, u].reshape(256, 128), NN)
         to_lon(s, send1)
@@ -268,7 +280,7 @@
             halves[128:256, columns(c, 128)] = low
             return carry
 
-        lax.fori_loop(0, 8, turn, 0)
+        repeat(8, turn)
 
     def lon_first(s):
         whole_l(1, s, send1, recv1).wait_recv()
@@ -291,37 +303,36 @@
             halves[128:256, columns(n, 256)] = low
             return carry
 
-        lax.fori_loop(0, 4, halve, 0)
+        repeat(4, halve)
 
         def back_block(n, carry):
             both = dot(halves[...], lonfull[:, columns(n, 256)], NN)
             summed = both[0:128] + both[128:256]
             for part in range(2):
                 rows = pl.ds(pl.multiple_of(n * 256 + part * 128, 128), 128)
-                send2[s, rows, :] = summed[:, part * 128 : (part + 1) * 128].T
-            return carry
-
-        lax.fori_loop(0, 4, back_block, 0)
+                send2[s, rows, :] = summed[:, part * 128 : (part + 1) * 128].T.astype(BF16)
+            return carry
+
+        repeat(4, back_block)
         start_l(2, s, send2, recv2)
 
     def lat_back(s):
         whole_l(2, s, send2, recv2).wait_recv()
+        ssc[...] = recv2[s].astype(F32)
 
         def swap(step, carry):
             u, lb = step // 2, step % 2
-            parts = [recv2[s, pl.ds(lb * 512 + u * 8 + pg, 16, stride=32), :] for pg in range(8)]
+            parts = [ssc[pl.ds(lb * 512 + u * 8 + pg, 16, stride=32), :] for pg in range(8)]
             parts = exchange(parts, (1, 2, 4))
             for k in range(8):
-                high, low = split(parts[k])
                 rows = pl.ds(pl.multiple_of(k * 32 + lb * 16, 16), 16)
-                xd[0, rows, columns(u, 128)] = high
-                xd[1, rows, columns(u, 128)] = low
-            return carry
-
-        lax.fori_loop(0, 8, swap, 0)
+                xd[rows, columns(u, 128)] = parts[k].astype(BF16)
+            return carry
+
+        repeat(8, swap)
         for n in range(2):
             cols = slice(n * 256, (n + 1) * 256)
-            ysc[:, cols] = dot(latqt[...], xd[0, :, cols], NN) + dot(latqt[...], xd[1, :, cols], NN)
+            ysc[:, cols] = dot(latqt[...], xd[:, cols], NN)
 
         def turn(step, carry):
             u, ib = step // 2, step % 2
@@ -331,14 +342,14 @@
                 ssc[pl.ds(pl.multiple_of((u * 16 + h) * 16 + ib * 8, 8), 8), :] = parts[h]
             return carry
 
-        lax.fori_loop(0, 8, turn, 0)
+        repeat(8, turn)
 
         def pick(peer, carry):
             for u in range(4):
                 send3[s, peer, u] = ssc[pl.ds(u * 256 + peer, 16, stride=16), :].astype(BF16)
             return carry
 
-        lax.fori_loop(0, ZN, pick, 0)
+        repeat(ZN, pick)
         start_z(3, s, send3, recv3)
 
     def hours_mix(s):
@@ -394,19 +405,19 @@
             ssc[pl.ds(pl.multiple_of(i * 64, 64), 64), :] = recv4[s, i].reshape(64, 128).astype(F32)
             return carry
 
-        lax.fori_loop(0, ZN, widen, 0)
+        repeat(ZN, widen)
 
         def turn(u, carry):
             parts = [ssc[pl.ds(u * 16 + h, 16, stride=64), :] for h in range(16)]
             parts = exchange(parts, (8, 16, 32, 64))
             for bb in range(16):
-                xd[0, pl.ds(bb * 16, 16), columns(u, 128)] = parts[bb].astype(BF16)
-            return carry
-
-        lax.fori_loop(0, 4, turn, 0)
+                xd[pl.ds(bb * 16, 16), columns(u, 128)] = parts[bb].astype(BF16)
+            return carry
+
+        repeat(4, turn)
         for n in range(2):
             cols = slice(n * 256, (n + 1) * 256)
-            ysc[:, cols] = dot(latq[...], xd[0, :, cols], NN)
+            ysc[:, cols] = dot(latq[...], xd[:, cols], NN)
         to_lon(s, send5)
         start_l(5, s, send5, recv5)
 
@@ -428,7 +439,7 @@
             nxt[s, :, columns(n, 256)] = left - step_size * operated
             return carry
 
-        lax.fori_loop(0, 4, block, 0)
+        repeat(4, block)
 
     lat_first(0)
     gathered.wait_recv()
@@ -470,10 +481,16 @@
     coarse = jnp.asarray(trig(16, 512, 16, 512))
     fine = jnp.asarray(trig(1, 512, 16, 512))
     vmem = pl.BlockSpec(memory_space=pltpu.VMEM)
-    anywhere = pl.BlockSpec(memory_space=pl.ANY)
+    hbm = pl.BlockSpec(memory_space=pltpu.HBM)
     zbuf = pltpu.VMEM((2, 16, 4, 16, 128), BF16)
     lbuf = pltpu.VMEM((2, 1024, 128), F32)
+    lhalf = pltpu.VMEM((2, 1024, 128), BF16)
     scratch = [
+        pltpu.VMEM((2, 16, 32, 512), BF16),
+        pltpu.VMEM((256, 256), BF16),
+        pltpu.VMEM((32, 1024), BF16),
+        pltpu.VMEM((32, 512), F32),
+        pltpu.VMEM((32, 512), F32),
         pltpu.VMEM((128, 1024), F32),
         pltpu.VMEM((128, 1024), jnp.int32),
         pltpu.VMEM((2, 2, 128, 1024), BF16),
@@ -488,27 +505,27 @@
         pltpu.VMEM((512, 256), BF16),
         pltpu.VMEM((1024, 1024), BF16),
         pltpu.VMEM((256, 1024), BF16),
-        pltpu.VMEM((2, 256, 512), BF16),
+        pltpu.VMEM((256, 512), BF16),
         pltpu.VMEM((2, 128, 1024), F32),
         pltpu.VMEM((2, 128, 1024), F32),
-        zbuf, zbuf, lbuf, lbuf, lbuf, lbuf, zbuf, zbuf, zbuf, zbuf, lbuf, lbuf,
+        zbuf, zbuf, lbuf, lbuf, lhalf, lhalf, zbuf, zbuf, zbuf, zbuf, lbuf, lbuf,
         pltpu.VMEM((2, 8, 128), F32),
         pltpu.VMEM((2, 16, 8, 128), F32),
         pltpu.VMEM((2, 8, 128), F32),
         pltpu.VMEM((2, 32, 8, 128), F32),
         pltpu.SemaphoreType.DMA((HOPS, 2)),
         pltpu.SemaphoreType.DMA((HOPS, 2)),
-        pltpu.SemaphoreType.DMA((4,)),
+        pltpu.SemaphoreType.DMA((9,)),
     ]
     out = jax.ShapeDtypeStruct((2, 128, 1024), F32)
     post, nxt = pl.pallas_call(
         body,
         out_shape=(out, out),
-        in_specs=[vmem, anywhere, anywhere, vmem, vmem, vmem, vmem, vmem],
+        in_specs=[hbm] * 5 + [vmem] + [hbm] * 2,
         out_specs=(vmem, vmem),
         scratch_shapes=scratch,
         compiler_params=pltpu.CompilerParams(
-            collective_id=0, has_side_effects=True, vmem_limit_bytes=50 << 20
+            collective_id=0, has_side_effects=True, vmem_limit_bytes=44 << 20
         ),
         name="posterior",
     )(

time: 166 us -> 147 us (0.89)
  Pallas kernels: 157 us -> 137 us
    pallas_call x1, Pallas kernels: 157 us -> 137 us  [shards(): pl.pallas_call(body, out_shape=(out, out), in_specs=[hbm] * 5 + [vmem] +...]
    unnamed x18 -> x20, local copies, waits for them, and re-layouts: 8.29 us -> 9.52 us
where the time goes in v2:
time: 147 us
  Pallas kernels  137 us (93%)
  local copies, waits for them, and re-layouts  9.59 us (7%)
    pallas_call x1, Pallas kernels, shards(): pl.pallas_call(body, out_shape=(out, out), in_specs=[hbm] * 5 + [vmem] +...  137 us
    unnamed x20, local copies, waits for them, and re-layouts  9.52 us

profile of v2, /device:TPU:1, one launch (start us, length us, event | category | flops | bytes accessed | tf_op | source)
XLA Modules:
  0.0 146.9 jit_solution(14827277441474891949)
XLA Ops:
  0.6 0.0 copy-start.7
  0.6 0.7 copy-done.7
  1.3 0.1 slice.3
  1.4 0.1 reverse
  1.5 0.1 slice.4
  1.6 0.1 fusion.amp
  1.6 0.0 copy-start
  1.6 1.2 copy-done
  2.9 0.0 copy-start.1
  2.9 1.0 copy-done.1
  3.9 0.0 copy-start.2
  3.9 1.0 copy-done.2
  5.0 0.0 copy-start.3
  5.0 0.9 copy-done.3
  5.9 0.0 copy-start.4
  5.9 0.8 copy-done.4
  6.7 0.0 copy-start.5
  6.7 0.8 copy-done.5
  7.5 0.0 copy-start.6
  7.5 0.8 copy-done.6
  8.4 136.5 %posterior.1 = (f32[2,128,1024]{2,1,0:T(8,128)S(1)}, f32[2,128,1024]{2,1,0:T(8,128)S(1)}) custom-call(bf16[2,16,32,512]{3,2,1,0:T(8,128)(2,1)S(1)} %copy-done, f32[128,1024]{1,0:T(8,128)S(1)} %bitcast.8, s32[128,1024]{1,0:T(8,128)S(1)} %bitcast.9, bf16[256,256]{1,0:T(8,128)(2,1)S(1)} %copy-done.3, bf16[32,1024]{1,0:T(8,128)(2,1)S(1)} %copy-done.4, ...), custom_call_target="tpu_custom_call" | custom-call | tf_op jit(solution)/shard_map/posterior/pallas_call | solution.py:521
  144.9 1.0 copy.12
  145.9 1.0 copy.13
  (1 shorter events, 0.0 us)
Async XLA Ops:
  0.6 0.7 copy-start.7
  1.6 1.2 copy-start
  2.9 1.0 copy-start.1
  3.9 1.0 copy-start.2
  5.0 0.9 copy-start.3
  5.9 0.8 copy-start.4
  6.7 0.8 copy-start.5
  7.5 0.8 copy-start.6

commit v3 on v2

--- a/solution.py
+++ b/solution.py
@@ -54,13 +54,13 @@
     lonfull, halves, xd, prior, resid,
     send0, recv0, send1, recv1, send2, recv2, send3, recv3, send4, recv4, send5, recv5,
     redsend, redz, redmid, redl,
-    send_sem, recv_sem, local_sem,
+    send_sem, recv_sem, gather_send, gather_recv, local_sem,
 ):
     mz = lax.axis_index("tm")
     ml = lax.axis_index("lon")
 
     def z_peer(step):
-        away = (step // 2 + 1) * (1 - 2 * (step % 2))
+        away = (8 - (step + 1) // 2) * (1 - 2 * (step % 2))
         return lax.rem(mz + away + ZN, ZN)
 
     def l_peer(step):
@@ -88,14 +88,16 @@
     lax.fori_loop(0, ZN - 1, greet_z, 0)
     lax.fori_loop(0, LN - 1, greet_l, 0)
 
+    def send_z(hop, s, src, dst, peer):
+        pltpu.make_async_remote_copy(
+            src_ref=src.at[s, peer], dst_ref=dst.at[s, mz],
+            send_sem=send_sem.at[hop, s], recv_sem=recv_sem.at[hop, s],
+            device_id={"tm": peer}, device_id_type=MESH,
+        ).start()
+
     def start_z(hop, s, src, dst):
         def one(step, carry):
-            peer = z_peer(step)
-            pltpu.make_async_remote_copy(
-                src_ref=src.at[s, peer], dst_ref=dst.at[s, mz],
-                send_sem=send_sem.at[hop, s], recv_sem=recv_sem.at[hop, s],
-                device_id={"tm": peer}, device_id_type=MESH,
-            ).start()
+            send_z(hop, s, src, dst, z_peer(step))
             return carry
 
         lax.fori_loop(0, ZN - 1, one, 0)
@@ -108,20 +110,15 @@
             device_id={"tm": z_peer(0)}, device_id_type=MESH,
         )
 
-    def start_l(hop, s, src, dst):
-        def one(step, carry):
-            peer = l_peer(step)
-            pltpu.make_async_remote_copy(
-                src_ref=src.at[s, pl.ds(pl.multiple_of(peer * 32, 32), 32)],
-                dst_ref=dst.at[s, pl.ds(pl.multiple_of(ml * 32, 32), 32)],
-                send_sem=send_sem.at[hop, s], recv_sem=recv_sem.at[hop, s],
-                device_id={"lon": peer}, device_id_type=MESH,
-            ).start()
-            return carry
-
-        lax.fori_loop(0, LN - 1, one, 0)
-        own = pl.ds(pl.multiple_of(ml * 32, 32), 32)
-        dst[s, own] = src[s, own]
+    def peer_rows(peer):
+        return pl.ds(pl.multiple_of(peer * 32, 32), 32)
+
+    def send_l(hop, s, src, dst, peer):
+        pltpu.make_async_remote_copy(
+            src_ref=src.at[s, peer_rows(peer)], dst_ref=dst.at[s, peer_rows(ml)],
+            send_sem=send_sem.at[hop, s], recv_sem=recv_sem.at[hop, s],
+            device_id={"lon": peer}, device_id_type=MESH,
+        ).start()
 
     def whole_l(hop, s, src, dst):
         rows = pl.ds(0, (LN - 1) * 32)
@@ -221,30 +218,69 @@
     fetches[5].wait()
     fetches[6].wait()
 
+    lonfull[peer_rows(ml), :] = lon[...]
+    for kind in range(3):
+        rest = 1024 - 256 * (kind + 1)
+        lonfull[256 * kind : 256 * (kind + 1), 1024 - rest :] = jnp.zeros((256, rest), BF16)
     pl.semaphore_wait(barrier, ZN + LN - 2)
     start_z(0, 0, send0, recv0)
 
-    own_rows = pl.ds(pl.multiple_of(ml * 32, 32), 32)
-
-    def gather(step, carry):
-        pltpu.make_async_remote_copy(
-            src_ref=lon, dst_ref=lonfull.at[own_rows],
-            send_sem=local_sem.at[7], recv_sem=local_sem.at[8],
-            device_id={"lon": l_peer(step)}, device_id_type=MESH,
-        ).start()
-        return carry
-
-    lax.fori_loop(0, LN - 1, gather, 0)
-    lonfull[own_rows, :] = lon[...]
-    gathered = pltpu.make_async_remote_copy(
-        src_ref=lonfull.at[pl.ds(0, 31 * 32)], dst_ref=lonfull.at[pl.ds(0, 31 * 32)],
-        send_sem=local_sem.at[7], recv_sem=local_sem.at[8],
-        device_id={"lon": l_peer(0)}, device_id_type=MESH,
-    )
+    sibling = ml + 1 - 2 * lax.rem(ml, 2)
+    own_class = ml // 8
+
+    def gather_copy(kind, rows, peer, cross):
+        width = 256 * (kind + 1)
+        return pltpu.make_async_remote_copy(
+            src_ref=lonfull.at[rows, pl.ds(0, width)], dst_ref=lonfull.at[rows, pl.ds(0, width)],
+            send_sem=gather_send.at[cross, kind], recv_sem=gather_recv.at[cross, kind],
+            device_id={"lon": peer}, device_id_type=MESH,
+        )
+
+    def gather_whole(kind, cross, count):
+        rows = pl.ds(256 * kind, count * 32)
+        return gather_copy(kind, rows, sibling, cross)
+
+    for kind in range(4):
+
+        @pl.when(own_class == kind)
+        def _():
+            def one(step, carry):
+                gather_copy(kind, peer_rows(ml), lax.rem(ml + 2 * step + 2, LN), 0).start()
+                return carry
+
+            lax.fori_loop(0, LN // 2 - 1, one, 0)
+
+    def gather_forward():
+        for kind in range(4):
+
+            @pl.when(own_class == kind)
+            def _():
+                gather_whole(kind, 0, 3).wait_recv()
+
+            @pl.when(own_class != kind)
+            def _():
+                gather_whole(kind, 0, 4).wait_recv()
+
+            for chip in range(4):
+                gather_copy(kind, peer_rows(kind * 8 + chip * 2 + lax.rem(ml, 2)), sibling, 1).start()
+
+    def gather_finish():
+        for kind in range(4):
+            gather_whole(kind, 1, 4).wait_recv()
+
+    def gather_drain():
+        for kind in range(4):
+            gather_whole(kind, 1, 4).wait_send()
+
+            @pl.when(own_class == kind)
+            def _():
+                gather_whole(kind, 0, 8).wait_send()
+                gather_whole(kind, 0, 7).wait_send()
+
     def columns(index, width):
         return pl.ds(pl.multiple_of(index * width, width), width)
 
-    def to_lon(s, dst):
+    def to_lon(hop, s, src, dst):
         def swap(step, carry):
             u, lb = step // 2, step % 2
             parts = [
@@ -257,11 +293,14 @@
 
         repeat(8, swap)
 
-        def pick(peer, carry):
-            dst[s, pl.ds(pl.multiple_of(peer * 32, 32), 32), :] = ssc[pl.ds(peer, 32, stride=32), :]
-            return carry
-
-        repeat(LN, pick)
+        def pick(step, carry):
+            peer = l_peer(step)
+            src[s, peer_rows(peer), :] = ssc[pl.ds(peer, 32, stride=32), :]
+            send_l(hop, s, src, dst, peer)
+            return carry
+
+        repeat(LN - 1, pick)
+        dst[s, peer_rows(ml), :] = ssc[pl.ds(ml, 32, stride=32), :]
 
     def lat_first(s):
         whole_z(0, s, send0, recv0).wait_recv()
@@ -269,8 +308,7 @@
             start_z(0, 1, send0, recv0)
         for u in range(4):
             ysc[:, u * 128 : (u + 1) * 128] = dot(latp[...], recv0[s, :, u].reshape(256, 128), NN)
-        to_lon(s, send1)
-        start_l(1, s, send1, recv1)
+        to_lon(1, s, send1, recv1)
 
     def lon_columns(s, src):
         def turn(c, carry):
@@ -305,16 +343,20 @@
 
         repeat(4, halve)
 
-        def back_block(n, carry):
+        for step in range(4):
+            n = lax.rem(ml // 8 + step, 4)
             both = dot(halves[...], lonfull[:, columns(n, 256)], NN)
             summed = both[0:128] + both[128:256]
             for part in range(2):
                 rows = pl.ds(pl.multiple_of(n * 256 + part * 128, 128), 128)
                 send2[s, rows, :] = summed[:, part * 128 : (part + 1) * 128].T.astype(BF16)
-            return carry
-
-        repeat(4, back_block)
-        start_l(2, s, send2, recv2)
+
+            def one(k, carry):
+                send_l(2, s, send2, recv2, n * 8 + lax.rem(ml + k, 8))
+                return carry
+
+            lax.fori_loop(1 if step == 0 else 0, 8, one, 0)
+        recv2[s, peer_rows(ml), :] = send2[s, peer_rows(ml), :]
 
     def lat_back(s):
         whole_l(2, s, send2, recv2).wait_recv()
@@ -344,13 +386,19 @@
 
         repeat(8, turn)
 
-        def pick(peer, carry):
+        def picked(peer, u):
+            return ssc[pl.ds(u * 256 + peer, 16, stride=16), :].astype(BF16)
+
+        def pick(step, carry):
+            peer = z_peer(step)
             for u in range(4):
-                send3[s, peer, u] = ssc[pl.ds(u * 256 + peer, 16, stride=16), :].astype(BF16)
-            return carry
-
-        repeat(ZN, pick)
-        start_z(3, s, send3, recv3)
+                send3[s, peer, u] = picked(peer, u)
+            send_z(3, s, send3, recv3, peer)
+            return carry
+
+        repeat(ZN - 1, pick)
+        for u in range(4):
+            recv3[s, mz, u] = picked(mz, u)
 
     def hours_mix(s):
         whole_z(3, s, send3, recv3).wait_recv()
@@ -418,8 +466,7 @@
         for n in range(2):
             cols = slice(n * 256, (n + 1) * 256)
             ysc[:, cols] = dot(latq[...], xd[:, cols], NN)
-        to_lon(s, send5)
-        start_l(5, s, send5, recv5)
+        to_lon(5, s, send5, recv5)
 
     def lon_last(s):
         sums_whole(s).wait_recv()
@@ -435,14 +482,21 @@
             applied = both[0:128] + both[128:256]
             left = resid[s, :, columns(n, 256)]
             operated = mask[:, columns(n, 256)].astype(F32) * applied + NOISE_VAR * left
-            post[s, :, columns(n, 256)] = prior[s, :, columns(n, 256)] + step_size * applied
-            nxt[s, :, columns(n, 256)] = left - step_size * operated
+            prior[s, :, columns(n, 256)] += step_size * applied
+            resid[s, :, columns(n, 256)] = left - step_size * operated
             return carry
 
         repeat(4, block)
 
+    def results(s):
+        return [
+            pltpu.make_async_copy(src.at[s], dst.at[s], local_sem.at[9 + 2 * s + index])
+            for index, (src, dst) in enumerate([(prior, post), (resid, nxt)])
+        ]
+
     lat_first(0)
-    gathered.wait_recv()
+    gather_forward()
+    gather_finish()
     lon_first(0)
     lat_first(1)
     lat_back(0)
@@ -450,14 +504,18 @@
     lat_back(1)
     hours_mix(0)
     hours_mix(1)
+    lat_last(0)
     sums_lon(0)
     sums_lon(1)
-    lat_last(0)
+    lat_last(1)
     lon_last(0)
-    lat_last(1)
+    for copy in results(0):
+        copy.start()
     lon_last(1)
-
-    gathered.wait_send()
+    for copy in results(1):
+        copy.start()
+
+    gather_drain()
     for s in range(2):
         whole_z(0, s, send0, recv0).wait_send()
         whole_l(1, s, send1, recv1).wait_send()
@@ -467,6 +525,8 @@
         whole_l(5, s, send5, recv5).wait_send()
         whole_z(6, s, redz, redz).wait_send()
         sums_whole(s).wait_send()
+        for copy in results(s):
+            copy.wait()
 
 
 def trig(step, period, count, columns):
@@ -515,17 +575,19 @@
         pltpu.VMEM((2, 32, 8, 128), F32),
         pltpu.SemaphoreType.DMA((HOPS, 2)),
         pltpu.SemaphoreType.DMA((HOPS, 2)),
-        pltpu.SemaphoreType.DMA((9,)),
+        pltpu.SemaphoreType.DMA((2, 4)),
+        pltpu.SemaphoreType.DMA((2, 4)),
+        pltpu.SemaphoreType.DMA((13,)),
     ]
     out = jax.ShapeDtypeStruct((2, 128, 1024), F32)
     post, nxt = pl.pallas_call(
         body,
         out_shape=(out, out),
         in_specs=[hbm] * 5 + [vmem] + [hbm] * 2,
-        out_specs=(vmem, vmem),
+        out_specs=(hbm, hbm),
         scratch_shapes=scratch,
         compiler_params=pltpu.CompilerParams(
-            collective_id=0, has_side_effects=True, vmem_limit_bytes=44 << 20
+            collective_id=0, has_side_effects=True, vmem_limit_bytes=58 << 20
         ),
         name="posterior",
     )(

time: 147 us -> 124 us (0.84)
  Pallas kernels: 137 us -> 118 us
  local copies, waits for them, and re-layouts: 9.59 us -> 4.29 us
    pallas_call x1, Pallas kernels: 137 us -> 118 us  [shards(): pl.pallas_call(body, out_shape=(out, out), in_specs=[hbm] * 5 + [vmem] +...]
    unnamed x20 -> x8, local copies, waits for them, and re-layouts: 9.52 us -> 4.22 us
where the time goes in v3:
time: 124 us
  Pallas kernels  118 us (95%)
  local copies, waits for them, and re-layouts  4.29 us (3%)
    pallas_call x1, Pallas kernels, shards(): pl.pallas_call(body, out_shape=(out, out), in_specs=[hbm] * 5 + [vmem] +...  118 us
    unnamed x8, local copies, waits for them, and re-layouts  4.22 us

profile of v3, /device:TPU:1, one launch (start us, length us, event | category | flops | bytes accessed | tf_op | source)
XLA Modules:
  0.0 123.8 jit_solution(17594048034128135380)
XLA Ops:
  0.6 0.0 copy-start.1
  0.6 0.7 copy-done.1
  1.3 0.1 slice.3
  1.4 0.1 reverse
  1.5 0.1 slice.4
  1.6 0.7 fusion.amp
  2.2 118.2 %posterior.1 = (f32[2,128,1024]{2,1,0:T(8,128)}, f32[2,128,1024]{2,1,0:T(8,128)}) custom-call(bf16[2,16,32,512]{3,2,1,0:T(8,128)(2,1)} %noise_hbm.1, f32[128,1024]{1,0:T(8,128)} %bitcast.8, s32[128,1024]{1,0:T(8,128)} %bitcast.9, bf16[256,256]{1,0:T(8,128)(2,1)} %lat_hbm.1, bf16[32,1024]{1,0:T(8,128)(2,1)} %lon_hbm.1, f32[1,512]{1,0:T(1,128)} %fusion.amp, ...), custom_call_target="tpu_custom_call" | custom-call | tf_op jit(solution)/shard_map/posterior/pallas_call | solution.py:583
  120.4 0.0 copy-start
  120.4 2.4 %copy.12 = f32[2,16,8,1024]{3,2,1,0:T(8,128)} copy(f32[2,16,8,1024]{3,2,1,0:T(8,128)} %bitcast.7) | data formatting | bytes 2097152
  122.8 0.0 copy-done
  122.8 1.0 copy.13
  (1 shorter events, 0.0 us)
Async XLA Ops:
  0.6 0.7 copy-start.1
  120.4 2.4 %copy-start = (f32[2,128,1024]{2,1,0:T(8,128)S(1)}, f32[2,128,1024]{2,1,0:T(8,128)}, u32[]{:S(2)}) copy-start(f32[2,128,1024]{2,1,0:T(8,128)} %get-tuple-element.5) | copy-start | bytes 3145732

commit v4 on v3

--- a/solution.py
+++ b/solution.py
@@ -48,9 +48,9 @@
 
 
 def body(
-    noise_hbm, obs_hbm, mask_hbm, lat_hbm, lon_hbm, amp, coarse_hbm, fine_hbm,
+    noise_hbm, obs_hbm, mask_hbm, lat_hbm, lon_hbm, spec_hbm, coarse_hbm, fine_hbm,
     post, nxt,
-    noise, lat, lon, coarse, fine, obs, mask, tab, waves, work, ysc, ssc, lat32, latp, latq, latqt, hour,
+    noise, lat, lon, coarse, fine, spec, obs, mask, tab, waves, work, ysc, ssc, tsc, lat32, latp, latq, latqt, hour,
     lonfull, halves, xd, prior, resid,
     send0, recv0, send1, recv1, send2, recv2, send3, recv3, send4, recv4, send5, recv5,
     redsend, redz, redmid, redl,
@@ -69,7 +69,7 @@
     fetches = [
         pltpu.make_async_copy(src, dst, local_sem.at[index])
         for index, (src, dst) in enumerate(
-            [(coarse_hbm, coarse), (fine_hbm, fine), (noise_hbm, noise), (lat_hbm, lat), (lon_hbm, lon),
+            [(coarse_hbm, coarse), (fine_hbm, fine), (noise_hbm, noise), (lat_hbm, lat), (lon_hbm, lon), (spec_hbm, spec),
              (obs_hbm, obs), (mask_hbm, mask)]
         )
     ]
@@ -88,49 +88,55 @@
     lax.fori_loop(0, ZN - 1, greet_z, 0)
     lax.fori_loop(0, LN - 1, greet_l, 0)
 
-    def send_z(hop, s, src, dst, peer):
+    def send_z(hop, s, half, src, dst, peer):
         pltpu.make_async_remote_copy(
-            src_ref=src.at[s, peer], dst_ref=dst.at[s, mz],
-            send_sem=send_sem.at[hop, s], recv_sem=recv_sem.at[hop, s],
+            src_ref=src.at[s, half, peer], dst_ref=dst.at[s, half, mz],
+            send_sem=send_sem.at[hop, s, half], recv_sem=recv_sem.at[hop, s, half],
             device_id={"tm": peer}, device_id_type=MESH,
         ).start()
 
-    def start_z(hop, s, src, dst):
+    def start_z(hop, s, half, src, dst):
         def one(step, carry):
-            send_z(hop, s, src, dst, z_peer(step))
+            send_z(hop, s, half, src, dst, z_peer(step))
             return carry
 
         lax.fori_loop(0, ZN - 1, one, 0)
-        dst[s, mz] = src[s, mz]
-
-    def whole_z(hop, s, src, dst):
+        dst[s, half, mz] = src[s, half, mz]
+
+    def whole_z(hop, s, half, src, dst):
         return pltpu.make_async_remote_copy(
-            src_ref=src.at[s, pl.ds(0, ZN - 1)], dst_ref=dst.at[s, pl.ds(0, ZN - 1)],
-            send_sem=send_sem.at[hop, s], recv_sem=recv_sem.at[hop, s],
+            src_ref=src.at[s, half, pl.ds(0, ZN - 1)], dst_ref=dst.at[s, half, pl.ds(0, ZN - 1)],
+            send_sem=send_sem.at[hop, s, half], recv_sem=recv_sem.at[hop, s, half],
             device_id={"tm": z_peer(0)}, device_id_type=MESH,
         )
 
-    def peer_rows(peer):
-        return pl.ds(pl.multiple_of(peer * 32, 32), 32)
-
-    def send_l(hop, s, src, dst, peer):
+    def peer_rows(peer, count=32):
+        return pl.ds(pl.multiple_of(peer * count, count), count)
+
+    def send_l(hop, s, half, src, dst, peer):
+        count = src.shape[2] // LN
         pltpu.make_async_remote_copy(
-            src_ref=src.at[s, peer_rows(peer)], dst_ref=dst.at[s, peer_rows(ml)],
-            send_sem=send_sem.at[hop, s], recv_sem=recv_sem.at[hop, s],
+            src_ref=src.at[s, half, peer_rows(peer, count)], dst_ref=dst.at[s, half, peer_rows(ml, count)],
+            send_sem=send_sem.at[hop, s, half], recv_sem=recv_sem.at[hop, s, half],
             device_id={"lon": peer}, device_id_type=MESH,
         ).start()
 
-    def whole_l(hop, s, src, dst):
-        rows = pl.ds(0, (LN - 1) * 32)
+    def whole_l(hop, s, half, src, dst):
+        rows = pl.ds(0, src.shape[2] // LN * (LN - 1))
         return pltpu.make_async_remote_copy(
-            src_ref=src.at[s, rows], dst_ref=dst.at[s, rows],
-            send_sem=send_sem.at[hop, s], recv_sem=recv_sem.at[hop, s],
+            src_ref=src.at[s, half, rows], dst_ref=dst.at[s, half, rows],
+            send_sem=send_sem.at[hop, s, half], recv_sem=recv_sem.at[hop, s, half],
             device_id={"lon": l_peer(0)}, device_id_type=MESH,
         )
 
-    for fetch in fetches[:5]:
+    for fetch in fetches[:6]:
         fetch.wait()
-    amp_row = amp[...]
+    order = lax.broadcasted_iota(jnp.int32, (257, 512), 1)
+    picks = (jnp.minimum(order, 512 - order) == lax.broadcasted_iota(jnp.int32, (257, 512), 0)).astype(F32)
+    powers = lax.dot_general(
+        spec[...].reshape(1, 257), picks, NN, precision=lax.Precision.HIGHEST, preferred_element_type=F32
+    )
+    amp_row = jnp.sqrt(powers / 512)
 
     def tables(group):
         base = pl.multiple_of(group * 8, 8)
@@ -170,7 +176,7 @@
                 parts = [work[pl.ds(u * 8 + og, 16, stride=32), :] for og in range(8)]
                 parts = exchange(parts, (1, 2, 4))
                 for jl in range(8):
-                    send0[s, group * 8 + jl, u] = parts[jl].astype(BF16)
+                    send0[s, u // 2, group * 8 + jl, u % 2] = parts[jl].astype(BF16)
                 return inner
 
             repeat(4, swap)
@@ -215,15 +221,16 @@
     hour[0:256, :] = high
     hour[256:512, :] = low
     redsend[...] = jnp.zeros_like(redsend)
-    fetches[5].wait()
     fetches[6].wait()
+    fetches[7].wait()
 
     lonfull[peer_rows(ml), :] = lon[...]
     for kind in range(3):
         rest = 1024 - 256 * (kind + 1)
         lonfull[256 * kind : 256 * (kind + 1), 1024 - rest :] = jnp.zeros((256, rest), BF16)
     pl.semaphore_wait(barrier, ZN + LN - 2)
-    start_z(0, 0, send0, recv0)
+    start_z(0, 0, 0, send0, recv0)
+    start_z(0, 0, 1, send0, recv0)
 
     sibling = ml + 1 - 2 * lax.rem(ml, 2)
     own_class = ml // 8
@@ -280,39 +287,41 @@
     def columns(index, width):
         return pl.ds(pl.multiple_of(index * width, width), width)
 
-    def to_lon(hop, s, src, dst):
+    def to_lon(hop, s, half, src, dst):
         def swap(step, carry):
-            u, lb = step // 2, step % 2
+            v, lb = step // 2, step % 2
             parts = [
-                ysc[pl.ds(pl.multiple_of(k * 32 + lb * 16, 16), 16), columns(u, 128)] for k in range(8)
+                ysc[pl.ds(pl.multiple_of(k * 32 + lb * 16, 16), 16), columns(v, 128)] for k in range(8)
             ]
             parts = exchange(parts, (1, 2, 4))
             for og in range(8):
-                ssc[pl.ds(pl.multiple_of((u * 8 + og) * 32 + lb * 16, 16), 16), :] = parts[og]
-            return carry
-
-        repeat(8, swap)
+                ssc[pl.ds(pl.multiple_of((v * 8 + og) * 32 + lb * 16, 16), 16), :] = parts[og]
+            return carry
+
+        repeat(4, swap)
 
         def pick(step, carry):
             peer = l_peer(step)
-            src[s, peer_rows(peer), :] = ssc[pl.ds(peer, 32, stride=32), :]
-            send_l(hop, s, src, dst, peer)
+            src[s, half, peer_rows(peer, 16), :] = ssc[pl.ds(peer, 16, stride=32), :]
+            send_l(hop, s, half, src, dst, peer)
             return carry
 
         repeat(LN - 1, pick)
-        dst[s, peer_rows(ml), :] = ssc[pl.ds(ml, 32, stride=32), :]
-
-    def lat_first(s):
-        whole_z(0, s, send0, recv0).wait_recv()
+        dst[s, half, peer_rows(ml, 16), :] = ssc[pl.ds(ml, 16, stride=32), :]
+
+    def lat_first(s, half):
+        whole_z(0, s, half, send0, recv0).wait_recv()
         if s == 0:
-            start_z(0, 1, send0, recv0)
-        for u in range(4):
-            ysc[:, u * 128 : (u + 1) * 128] = dot(latp[...], recv0[s, :, u].reshape(256, 128), NN)
-        to_lon(1, s, send1, recv1)
+            start_z(0, 1, half, send0, recv0)
+        cells = jnp.concatenate([recv0[s, half, :, v].reshape(256, 128) for v in range(2)], axis=1)
+        ysc[...] = dot(latp[...], cells, NN)
+        to_lon(1, s, half, send1, recv1)
 
     def lon_columns(s, src):
         def turn(c, carry):
-            block = src[s, columns(c, 128), :].T
+            block = jnp.concatenate(
+                [src[s, half, peer_rows(c * 4 + i, 16), :] for i in range(4) for half in range(2)], axis=0
+            ).T
             high, low = split(block)
             halves[0:128, columns(c, 128)] = high
             halves[128:256, columns(c, 128)] = low
@@ -321,7 +330,8 @@
         repeat(8, turn)
 
     def lon_first(s):
-        whole_l(1, s, send1, recv1).wait_recv()
+        for half in range(2):
+            whole_l(1, s, half, send1, recv1).wait_recv()
         lon_columns(s, recv1)
 
         def prior_block(n, total):
@@ -349,89 +359,100 @@
             summed = both[0:128] + both[128:256]
             for part in range(2):
                 rows = pl.ds(pl.multiple_of(n * 256 + part * 128, 128), 128)
-                send2[s, rows, :] = summed[:, part * 128 : (part + 1) * 128].T.astype(BF16)
+                send2[s, 0, rows, :] = summed[:, part * 128 : (part + 1) * 128].T.astype(BF16)
 
             def one(k, carry):
-                send_l(2, s, send2, recv2, n * 8 + lax.rem(ml + k, 8))
+                send_l(2, s, 0, send2, recv2, n * 8 + lax.rem(ml + k, 8))
                 return carry
 
             lax.fori_loop(1 if step == 0 else 0, 8, one, 0)
-        recv2[s, peer_rows(ml), :] = send2[s, peer_rows(ml), :]
+        recv2[s, 0, peer_rows(ml), :] = send2[s, 0, peer_rows(ml), :]
 
     def lat_back(s):
-        whole_l(2, s, send2, recv2).wait_recv()
-        ssc[...] = recv2[s].astype(F32)
-
-        def swap(step, carry):
-            u, lb = step // 2, step % 2
-            parts = [ssc[pl.ds(lb * 512 + u * 8 + pg, 16, stride=32), :] for pg in range(8)]
-            parts = exchange(parts, (1, 2, 4))
-            for k in range(8):
-                rows = pl.ds(pl.multiple_of(k * 32 + lb * 16, 16), 16)
-                xd[rows, columns(u, 128)] = parts[k].astype(BF16)
-            return carry
-
-        repeat(8, swap)
-        for n in range(2):
-            cols = slice(n * 256, (n + 1) * 256)
-            ysc[:, cols] = dot(latqt[...], xd[:, cols], NN)
-
-        def turn(step, carry):
-            u, ib = step // 2, step % 2
-            parts = [ysc[pl.ds(pl.multiple_of(bb * 16 + ib * 8, 8), 8), columns(u, 128)] for bb in range(16)]
-            parts = exchange(parts, (8, 16, 32, 64))
-            for h in range(16):
-                ssc[pl.ds(pl.multiple_of((u * 16 + h) * 16 + ib * 8, 8), 8), :] = parts[h]
-            return carry
-
-        repeat(8, turn)
-
-        def picked(peer, u):
-            return ssc[pl.ds(u * 256 + peer, 16, stride=16), :].astype(BF16)
-
-        def pick(step, carry):
-            peer = z_peer(step)
-            for u in range(4):
-                send3[s, peer, u] = picked(peer, u)
-            send_z(3, s, send3, recv3, peer)
-            return carry
-
-        repeat(ZN - 1, pick)
-        for u in range(4):
-            recv3[s, mz, u] = picked(mz, u)
-
-    def hours_mix(s):
-        whole_z(3, s, send3, recv3).wait_recv()
-        total = jnp.zeros((1, 128), F32)
-        for u in range(4):
-            cells = recv3[s, :, u].reshape(256, 128)
-            both = dot(hour[...], cells, NN)
-            mixed = both[0:256] + both[256:512]
-            total = total + jnp.sum(mixed * cells.astype(F32), axis=0, keepdims=True)
-            send4[s, :, u] = mixed.astype(BF16).reshape(16, 16, 128)
-        redsend[s, 1:2, :] = total
-
-        def one(step, carry):
-            peer = z_peer(step)
-            pltpu.make_async_remote_copy(
-                src_ref=redsend.at[s], dst_ref=redz.at[s, mz],
-                send_sem=send_sem.at[6, s], recv_sem=recv_sem.at[6, s],
-                device_id={"tm": peer}, device_id_type=MESH,
-            ).start()
-            return carry
-
-        lax.fori_loop(0, ZN - 1, one, 0)
-        redz[s, mz] = redsend[s]
-        start_z(4, s, send4, recv4)
+        whole_l(2, s, 0, send2, recv2).wait_recv()
+        ssc[...] = recv2[s, 0].astype(F32)
+        for half in range(2):
+
+            def swap(step, carry):
+                v, lb = step // 2, step % 2
+                base = lb * 512 + half * 16 + v * 8
+                parts = [ssc[pl.ds(base + pg, 16, stride=32), :] for pg in range(8)]
+                parts = exchange(parts, (1, 2, 4))
+                for k in range(8):
+                    rows = pl.ds(pl.multiple_of(k * 32 + lb * 16, 16), 16)
+                    xd[rows, columns(v, 128)] = parts[k].astype(BF16)
+                return carry
+
+            repeat(4, swap)
+            ysc[...] = dot(latqt[...], xd[...], NN)
+
+            def turn(step, carry):
+                v, ib = step // 2, step % 2
+                parts = [
+                    ysc[pl.ds(pl.multiple_of(bb * 16 + ib * 8, 8), 8), columns(v, 128)] for bb in range(16)
+                ]
+                parts = exchange(parts, (8, 16, 32, 64))
+                for h in range(16):
+                    tsc[pl.ds(pl.multiple_of((v * 16 + h) * 16 + ib * 8, 8), 8), :] = parts[h]
+                return carry
+
+            repeat(4, turn)
+
+            def picked(peer, v):
+                return tsc[pl.ds(v * 256 + peer, 16, stride=16), :].astype(BF16)
+
+            def pick(step, carry):
+                peer = z_peer(step)
+                for v in range(2):
+                    send3[s, half, peer, v] = picked(peer, v)
+                send_z(3, s, half, send3, recv3, peer)
+                return carry
+
+            repeat(ZN - 1, pick)
+            for v in range(2):
+                recv3[s, half, mz, v] = picked(mz, v)
+
+    quads = {}
+
+    def hours_mix(s, half):
+        whole_z(3, s, half, send3, recv3).wait_recv()
+        cells = jnp.concatenate([recv3[s, half, :, v].reshape(256, 128) for v in range(2)], axis=1)
+        both = dot(hour[...], cells, NN)
+        mixed = both[0:256] + both[256:512]
+        total = jnp.sum(mixed * cells.astype(F32), axis=0, keepdims=True)
+        quads[s, half] = total[:, 0:128] + total[:, 128:256]
+        for v in range(2):
+            send4[s, half, :, v] = mixed[:, v * 128 : (v + 1) * 128].astype(BF16).reshape(16, 16, 128)
+        if half == 1:
+            redsend[s, 1:2, :] = quads[s, 0] + quads[s, 1]
+
+            def one(step, carry):
+                pltpu.make_async_remote_copy(
+                    src_ref=redsend.at[s], dst_ref=redz.at[s, mz],
+                    send_sem=send_sem.at[6, s, 0], recv_sem=recv_sem.at[6, s, 0],
+                    device_id={"tm": z_peer(step)}, device_id_type=MESH,
+                ).start()
+                return carry
+
+            lax.fori_loop(0, ZN - 1, one, 0)
+            redz[s, mz] = redsend[s]
+        start_z(4, s, half, send4, recv4)
+
+    def sums_z_whole(s):
+        part = redz.at[s, pl.ds(0, ZN - 1)]
+        return pltpu.make_async_remote_copy(
+            src_ref=part, dst_ref=part, send_sem=send_sem.at[6, s, 0], recv_sem=recv_sem.at[6, s, 0],
+            device_id={"tm": z_peer(0)}, device_id_type=MESH,
+        )
 
     def sums_lon(s):
-        whole_z(6, s, redz, redz).wait_recv()
+        sums_z_whole(s).wait_recv()
         redmid[s] = jnp.sum(redz[s], axis=0)
 
         def one(step, carry):
             pltpu.make_async_remote_copy(
                 src_ref=redmid.at[s], dst_ref=redl.at[s, ml],
-                send_sem=send_sem.at[7, s], recv_sem=recv_sem.at[7, s],
+                send_sem=send_sem.at[7, s, 0], recv_sem=recv_sem.at[7, s, 0],
                 device_id={"lon": l_peer(step)}, device_id_type=MESH,
             ).start()
             return carry
@@ -442,31 +463,29 @@
     def sums_whole(s):
         part = redl.at[s, pl.ds(0, LN - 1)]
         return pltpu.make_async_remote_copy(
-            src_ref=part, dst_ref=part, send_sem=send_sem.at[7, s], recv_sem=recv_sem.at[7, s],
+            src_ref=part, dst_ref=part, send_sem=send_sem.at[7, s, 0], recv_sem=recv_sem.at[7, s, 0],
             device_id={"lon": l_peer(0)}, device_id_type=MESH,
         )
 
-    def lat_last(s):
-        whole_z(4, s, send4, recv4).wait_recv()
+    def lat_last(s, half):
+        whole_z(4, s, half, send4, recv4).wait_recv()
 
         def widen(i, carry):
-            ssc[pl.ds(pl.multiple_of(i * 64, 64), 64), :] = recv4[s, i].reshape(64, 128).astype(F32)
+            ssc[peer_rows(i), :] = recv4[s, half, i].reshape(32, 128).astype(F32)
             return carry
 
         repeat(ZN, widen)
 
-        def turn(u, carry):
-            parts = [ssc[pl.ds(u * 16 + h, 16, stride=64), :] for h in range(16)]
+        def turn(v, carry):
+            parts = [ssc[pl.ds(v * 16 + h, 16, stride=32), :] for h in range(16)]
             parts = exchange(parts, (8, 16, 32, 64))
             for bb in range(16):
-                xd[pl.ds(bb * 16, 16), columns(u, 128)] = parts[bb].astype(BF16)
-            return carry
-
-        repeat(4, turn)
-        for n in range(2):
-            cols = slice(n * 256, (n + 1) * 256)
-            ysc[:, cols] = dot(latq[...], xd[:, cols], NN)
-        to_lon(5, s, send5, recv5)
+                xd[pl.ds(bb * 16, 16), columns(v, 128)] = parts[bb].astype(BF16)
+            return carry
+
+        repeat(2, turn)
+        ysc[...] = dot(latq[...], xd[...], NN)
+        to_lon(5, s, half, send5, recv5)
 
     def lon_last(s):
         sums_whole(s).wait_recv()
@@ -474,7 +493,8 @@
         norm_sq = jnp.sum(total[0:1], axis=1, keepdims=True)
         quad = jnp.sum(total[1:2], axis=1, keepdims=True)
         step_size = norm_sq / (quad + NOISE_VAR * norm_sq)
-        whole_l(5, s, send5, recv5).wait_recv()
+        for half in range(2):
+            whole_l(5, s, half, send5, recv5).wait_recv()
         lon_columns(s, recv5)
 
         def block(n, carry):
@@ -490,40 +510,47 @@
 
     def results(s):
         return [
-            pltpu.make_async_copy(src.at[s], dst.at[s], local_sem.at[9 + 2 * s + index])
+            pltpu.make_async_copy(src.at[s], dst.at[s], local_sem.at[10 + 2 * s + index])
             for index, (src, dst) in enumerate([(prior, post), (resid, nxt)])
         ]
 
-    lat_first(0)
+    lat_first(0, 0)
+    lat_first(0, 1)
     gather_forward()
     gather_finish()
     lon_first(0)
-    lat_first(1)
+    lat_first(1, 0)
+    lat_first(1, 1)
     lat_back(0)
     lon_first(1)
+    hours_mix(0, 0)
     lat_back(1)
-    hours_mix(0)
-    hours_mix(1)
-    lat_last(0)
+    hours_mix(0, 1)
+    hours_mix(1, 0)
+    hours_mix(1, 1)
+    lat_last(0, 0)
+    lat_last(0, 1)
     sums_lon(0)
     sums_lon(1)
-    lat_last(1)
+    lat_last(1, 0)
     lon_last(0)
     for copy in results(0):
         copy.start()
+    lat_last(1, 1)
     lon_last(1)
     for copy in results(1):
         copy.start()
 
     gather_drain()
     for s in range(2):
-        whole_z(0, s, send0, recv0).wait_send()
-        whole_l(1, s, send1, recv1).wait_send()
-        whole_l(2, s, send2, recv2).wait_send()
-        whole_z(3, s, send3, recv3).wait_send()
-        whole_z(4, s, send4, recv4).wait_send()
-        whole_l(5, s, send5, recv5).wait_send()
-        whole_z(6, s, redz, redz).wait_send()
+        for half in range(2):
+            whole_z(0, s, half, send0, recv0).wait_send()
+            whole_l(1, s, half, send1, recv1).wait_send()
+            whole_z(3, s, half, send3, recv3).wait_send()
+            whole_z(4, s, half, send4, recv4).wait_send()
+            whole_l(5, s, half, send5, recv5).wait_send()
+        whole_l(2, s, 0, send2, recv2).wait_send()
+        sums_z_whole(s).wait_send()
         sums_whole(s).wait_send()
         for copy in results(s):
             copy.wait()
@@ -536,28 +563,28 @@
 
 def shards(noise, observed, mask, lat_factor, lon_factor, spectrum):
     periods = noise.shape[3]
-    powers = jnp.concatenate([spectrum, spectrum[1:-1][::-1]])
-    amplitude = jnp.sqrt(powers / periods)[None]
     coarse = jnp.asarray(trig(16, 512, 16, 512))
     fine = jnp.asarray(trig(1, 512, 16, 512))
     vmem = pl.BlockSpec(memory_space=pltpu.VMEM)
     hbm = pl.BlockSpec(memory_space=pltpu.HBM)
-    zbuf = pltpu.VMEM((2, 16, 4, 16, 128), BF16)
-    lbuf = pltpu.VMEM((2, 1024, 128), F32)
-    lhalf = pltpu.VMEM((2, 1024, 128), BF16)
+    zbuf = pltpu.VMEM((2, 2, 16, 2, 16, 128), BF16)
+    lbuf = pltpu.VMEM((2, 2, 512, 128), F32)
+    lhalf = pltpu.VMEM((2, 1, 1024, 128), BF16)
     scratch = [
         pltpu.VMEM((2, 16, 32, 512), BF16),
         pltpu.VMEM((256, 256), BF16),
         pltpu.VMEM((32, 1024), BF16),
         pltpu.VMEM((32, 512), F32),
         pltpu.VMEM((32, 512), F32),
+        pltpu.VMEM((257,), F32),
         pltpu.VMEM((128, 1024), F32),
         pltpu.VMEM((128, 1024), jnp.int32),
         pltpu.VMEM((2, 2, 128, 1024), BF16),
         pltpu.VMEM((2, 256, 1024), BF16),
         pltpu.VMEM((512, 128), F32),
-        pltpu.VMEM((256, 512), F32),
+        pltpu.VMEM((256, 256), F32),
         pltpu.VMEM((1024, 128), F32),
+        pltpu.VMEM((512, 128), F32),
         pltpu.VMEM((512, 128), F32),
         pltpu.VMEM((256, 256), BF16),
         pltpu.VMEM((256, 256), BF16),
@@ -565,7 +592,7 @@
         pltpu.VMEM((512, 256), BF16),
         pltpu.VMEM((1024, 1024), BF16),
         pltpu.VMEM((256, 1024), BF16),
-        pltpu.VMEM((256, 512), BF16),
+        pltpu.VMEM((256, 256), BF16),
         pltpu.VMEM((2, 128, 1024), F32),
         pltpu.VMEM((2, 128, 1024), F32),
         zbuf, zbuf, lbuf, lbuf, lhalf, lhalf, zbuf, zbuf, zbuf, zbuf, lbuf, lbuf,
@@ -573,17 +600,17 @@
         pltpu.VMEM((2, 16, 8, 128), F32),
         pltpu.VMEM((2, 8, 128), F32),
         pltpu.VMEM((2, 32, 8, 128), F32),
-        pltpu.SemaphoreType.DMA((HOPS, 2)),
-        pltpu.SemaphoreType.DMA((HOPS, 2)),
+        pltpu.SemaphoreType.DMA((HOPS, 2, 2)),
+        pltpu.SemaphoreType.DMA((HOPS, 2, 2)),
         pltpu.SemaphoreType.DMA((2, 4)),
         pltpu.SemaphoreType.DMA((2, 4)),
-        pltpu.SemaphoreType.DMA((13,)),
+        pltpu.SemaphoreType.DMA((14,)),
     ]
     out = jax.ShapeDtypeStruct((2, 128, 1024), F32)
     post, nxt = pl.pallas_call(
         body,
         out_shape=(out, out),
-        in_specs=[hbm] * 5 + [vmem] + [hbm] * 2,
+        in_specs=[hbm] * 8,
         out_specs=(hbm, hbm),
         scratch_shapes=scratch,
         compiler_params=pltpu.CompilerParams(
@@ -591,7 +618,7 @@
         ),
         name="posterior",
     )(
-        noise, observed.reshape(128, 1024), mask.reshape(128, 1024), lat_factor, lon_factor, amplitude, coarse, fine
+        noise, observed.reshape(128, 1024), mask.reshape(128, 1024), lat_factor, lon_factor, spectrum, coarse, fine
     )
     return post.reshape(2, 16, 8, 1024), nxt.reshape(2, 16, 8, 1024)
 

time: 124 us -> 118 us (0.952)
  Pallas kernels: 118 us -> 114 us
    pallas_call x1, Pallas kernels: 118 us -> 114 us  [shards(): pl.pallas_call(body, out_shape=(out, out), in_specs=[hbm] * 8, out_specs=...]
    unnamed x8 -> x4, local copies, waits for them, and re-layouts: 4.22 us -> 3.37 us
where the time goes in v4:
time: 118 us
  Pallas kernels  114 us (97%)
  local copies, waits for them, and re-layouts  3.37 us (3%)
    pallas_call x1, Pallas kernels, shards(): pl.pallas_call(body, out_shape=(out, out), in_specs=[hbm] * 8, out_specs=...  114 us
    unnamed x4, local copies, waits for them, and re-layouts  3.37 us

profile of v4, /device:TPU:1, one launch (start us, length us, event | category | flops | bytes accessed | tf_op | source)
XLA Modules:
  0.0 118.2 jit_solution(11364777334115538308)
XLA Ops:
  0.6 114.2 %posterior.1 = (f32[2,128,1024]{2,1,0:T(8,128)}, f32[2,128,1024]{2,1,0:T(8,128)}) custom-call(bf16[2,16,32,512]{3,2,1,0:T(8,128)(2,1)} %noise_hbm.1, f32[128,1024]{1,0:T(8,128)} %bitcast.6, s32[128,1024]{1,0:T(8,128)} %bitcast.7, bf16[256,256]{1,0:T(8,128)(2,1)} %lat_hbm.1, bf16[32,1024]{1,0:T(8,128)(2,1)} %lon_hbm.1, f32[257]{0:T(512)} %spec_hbm.1, ...), custom_call_target="tpu_custom_call" | custom-call | tf_op jit(solution)/shard_map/posterior/pallas_call | solution.py:610
  114.8 0.0 copy-start
  114.8 2.4 %copy.12 = f32[2,16,8,1024]{3,2,1,0:T(8,128)} copy(f32[2,16,8,1024]{3,2,1,0:T(8,128)} %bitcast.5) | data formatting | bytes 2097152
  117.2 0.0 copy-done
  117.2 1.0 copy.13
Async XLA Ops:
  114.8 2.4 %copy-start = (f32[2,128,1024]{2,1,0:T(8,128)S(1)}, f32[2,128,1024]{2,1,0:T(8,128)}, u32[]{:S(2)}) copy-start(f32[2,128,1024]{2,1,0:T(8,128)} %get-tuple-element.5) | copy-start | bytes 3145732

commit v5 on v4

--- a/solution.py
+++ b/solution.py
@@ -100,7 +100,7 @@
             send_z(hop, s, half, src, dst, z_peer(step))
             return carry
 
-        lax.fori_loop(0, ZN - 1, one, 0)
+        lax.fori_loop(0, ZN - 1, one, 0, unroll=5)
         dst[s, half, mz] = src[s, half, mz]
 
     def whole_z(hop, s, half, src, dst):
@@ -334,16 +334,17 @@
             whole_l(1, s, half, send1, recv1).wait_recv()
         lon_columns(s, recv1)
 
-        def prior_block(n, total):
-            both = dot(halves[...], lonfull[columns(n, 256), :], NT)
+        squares = jnp.zeros((1, 128), F32)
+        for n in range(4):
+            cols = slice(n * 256, (n + 1) * 256)
+            both = dot(halves[:, : (n + 1) * 256], lonfull[cols, : (n + 1) * 256], NT)
             drawn = both[0:128] + both[128:256]
-            left = mask[:, columns(n, 256)].astype(F32) * (obs[:, columns(n, 256)] - drawn)
-            prior[s, :, columns(n, 256)] = drawn
-            resid[s, :, columns(n, 256)] = left
-            squares = jnp.sum(left * left, axis=0, keepdims=True)
-            return total + squares[:, 0:128] + squares[:, 128:256]
-
-        redsend[s, 0:1, :] = lax.fori_loop(0, 4, prior_block, jnp.zeros((1, 128), F32))
+            left = mask[:, cols].astype(F32) * (obs[:, cols] - drawn)
+            prior[s, :, cols] = drawn
+            resid[s, :, cols] = left
+            summed = jnp.sum(left * left, axis=0, keepdims=True)
+            squares = squares + summed[:, 0:128] + summed[:, 128:256]
+        redsend[s, 0:1, :] = squares
 
         def halve(n, carry):
             high, low = split(resid[s, :, columns(n, 256)])
@@ -365,7 +366,7 @@
                 send_l(2, s, 0, send2, recv2, n * 8 + lax.rem(ml + k, 8))
                 return carry
 
-            lax.fori_loop(1 if step == 0 else 0, 8, one, 0)
+            lax.fori_loop(1 if step == 0 else 0, 8, one, 0, unroll=True)
         recv2[s, 0, peer_rows(ml), :] = send2[s, 0, peer_rows(ml), :]
 
     def lat_back(s):
@@ -497,16 +498,18 @@
             whole_l(5, s, half, send5, recv5).wait_recv()
         lon_columns(s, recv5)
 
-        def block(n, carry):
-            both = dot(halves[...], lonfull[columns(n, 256), :], NT)
+        for n in range(4):
+            cols = slice(n * 256, (n + 1) * 256)
+            both = dot(halves[:, : (n + 1) * 256], lonfull[cols, : (n + 1) * 256], NT)
             applied = both[0:128] + both[128:256]
-            left = resid[s, :, columns(n, 256)]
-            operated = mask[:, columns(n, 256)].astype(F32) * applied + NOISE_VAR * left
-            prior[s, :, columns(n, 256)] += step_size * applied
-            resid[s, :, columns(n, 256)] = left - step_size * operated
-            return carry
-
-        repeat(4, block)
+            left = resid[s, :, cols]
+            operated = mask[:, cols].astype(F32) * applied + NOISE_VAR * left
+            prior[s, :, cols] += step_size * applied
+            resid[s, :, cols] = left - step_size * operated
+            for index, (held, result) in enumerate([(prior, post), (resid, nxt)]):
+                pltpu.make_async_copy(
+                    held.at[s, :, cols], result.at[s, :, cols], local_sem.at[10 + 2 * s + index]
+                ).start()
 
     def results(s):
         return [
@@ -531,15 +534,11 @@
     lat_last(0, 0)
     lat_last(0, 1)
     sums_lon(0)
+    lat_last(1, 0)
     sums_lon(1)
-    lat_last(1, 0)
     lon_last(0)
-    for copy in results(0):
-        copy.start()
     lat_last(1, 1)
     lon_last(1)
-    for copy in results(1):
-        copy.start()
 
     gather_drain()
     for s in range(2):

time: 118 us -> 117 us (level)
  Pallas kernels: 114 us -> 112 us
    pallas_call x1, Pallas kernels: 114 us -> 112 us  [shards(): pl.pallas_call(body, out_shape=(out, out), in_specs=[hbm] * 8, out_specs=...]
where the time goes in v5:
time: 117 us; the launch traced here: 116 us
  Pallas kernels  112 us (96%)
  local copies, waits for them, and re-layouts  3.37 us (3%)
    pallas_call x1, Pallas kernels, shards(): pl.pallas_call(body, out_shape=(out, out), in_specs=[hbm] * 8, out_specs=...  112 us
    unnamed x4, local copies, waits for them, and re-layouts  3.37 us

profile of v5, /device:TPU:1, one launch (start us, length us, event | category | flops | bytes accessed | tf_op | source)
XLA Modules:
  0.0 116.5 jit_solution(8105097450631239073)
XLA Ops:
  0.6 112.4 %posterior.1 = (f32[2,128,1024]{2,1,0:T(8,128)}, f32[2,128,1024]{2,1,0:T(8,128)}) custom-call(bf16[2,16,32,512]{3,2,1,0:T(8,128)(2,1)} %noise_hbm.1, f32[128,1024]{1,0:T(8,128)} %bitcast.6, s32[128,1024]{1,0:T(8,128)} %bitcast.7, bf16[256,256]{1,0:T(8,128)(2,1)} %lat_hbm.1, bf16[32,1024]{1,0:T(8,128)(2,1)} %lon_hbm.1, f32[257]{0:T(512)} %spec_hbm.1, ...), custom_call_target="tpu_custom_call" | custom-call | tf_op jit(solution)/shard_map/posterior/pallas_call | solution.py:609
  113.1 0.0 copy-start
  113.1 2.4 %copy.12 = f32[2,16,8,1024]{3,2,1,0:T(8,128)} copy(f32[2,16,8,1024]{3,2,1,0:T(8,128)} %bitcast.5) | data formatting | bytes 2097152
  115.5 0.0 copy-done
  115.5 1.0 copy.13
Async XLA Ops:
  113.1 2.4 %copy-start = (f32[2,128,1024]{2,1,0:T(8,128)S(1)}, f32[2,128,1024]{2,1,0:T(8,128)}, u32[]{:S(2)}) copy-start(f32[2,128,1024]{2,1,0:T(8,128)} %get-tuple-element.5) | copy-start | bytes 3145732
